TPU v7x, 256 devices: a whole 4x4x8 slice. The times are simulated.
256 devices in a mesh: pool: 8 (over z), tp: 32 (over x, y, core).
Axes of the slice: x: 4, y: 4, z: 8, core: 2. Of those that a mesh axis runs over, the one named last changes fastest.
Arguments:
- tokens: bfloat16 [4096, 8192], P(('pool', 'tp')), may hold values from -4 to 4
- lengths: int32 [8, 4], P('pool'), may hold values from 1 to 256, 512 in all within a row
- hit_pages: int32 [8, 4, 4], P('pool'), may hold values from 0 to 4095, as said below
- new_owner: int32 [8, 16], P('pool'), may hold values from 0 to 7, as said below
- w_query: bfloat16 [8192, 8192], P('pool', 'tp'), may hold values from -0.125 to 0.125
- w_keyval: bfloat16 [4096, 4096], P('pool', 'tp'), may hold values from -0.0625 to 0.0625
- w_out: bfloat16 [8192, 8192], P('tp', 'pool'), may hold values from -0.0625 to 0.0625
- pool_pages: bfloat16 [4096, 32, 2048], P('pool', 'tp'), may hold values from -65 to 65
Outputs:
- mixed: float32 [4096, 8192], P(('pool', 'tp'))
- new_store: bfloat16 [128, 32, 2048], P('pool', 'tp')
Inputs may be any that keep to these rules, and one draw needn't show every extreme that they name: Page p of the pool lies on pool index p // 512. In every group g at most 6 of the 16 entries of hit_pages[g] lie on one pool index, and some pool index holds exactly 6 of them in every group. A page may appear more than once. `new_owner`: in every group at most 2 of its 16 pages go to one pool index, and some pool index receives exactly 2 from every group. Row g holds the lengths of the 4 requests packed in group g, in order, and sums to 512.
All inputs are finite; a program needn't handle non-finite values.
Results may differ from a plain program's by a relative error of at most 0.009.
Values may be sent and summed in bfloat16 or wider, within the bound.
No kernel may reach another device: no remote copies, remote signals or barrier semaphores. Data moves between devices by JAX's collectives and lax.ppermute only.
A program may use at most 64 MiB of HBM per device.

v0:
```python
import math

import jax
import jax.numpy as jnp
from jax import lax
from jax.sharding import PartitionSpec as P

KVH = 8
HD = 128
PAGE = 32
REQS = 4
HITS = 4
CAPF = 6
CAPN = 2


EPSILON = 1e-06
ROPE_BASE = 1000000.0


def in_one_piece(arrays, axis, dim, along):
    ends, at = ([], 0)
    for a in arrays[:-1]:
        at += a.shape[along]
        ends.append(at)
    both = jnp.concatenate(arrays, axis=along)
    return tuple(jnp.split(lax.all_gather(both, axis, axis=dim, tiled=True), ends, axis=along))


def partner(value, axis, stride):
    mask = 2**stride
    pairs = [(source, source ^ mask) for source in range(lax.axis_size(axis))]
    return lax.ppermute(value, axis, pairs)


def rotate(values, positions):
    half = values.shape[-1] // 2
    steps_range = jnp.arange(half, dtype=jnp.float32)
    frequency = ROPE_BASE ** (-2.0 * steps_range / values.shape[-1])
    angles = positions.astype(jnp.float32)[:, None, None] * frequency[None, None, :]
    cosine = jnp.cos(angles)
    sine = jnp.sin(angles)
    first_half = values[..., :half]
    second_half = values[..., half:]
    return jnp.concatenate(
        [first_half * cosine - second_half * sine, second_half * cosine + first_half * sine],
        axis=-1,
    )


def slot_table(owners_row, capacity, seats):
    count_items = owners_row.shape[0]
    item_index = jnp.arange(count_items, dtype=jnp.int32)
    earlier_same = (owners_row[:, None] == owners_row[None, :]) & (
        item_index[None, :] < item_index[:, None]
    )
    slots = jnp.sum(earlier_same.astype(jnp.int32), axis=1)
    targets = owners_row * capacity + slots
    seat_index = jnp.arange(seats, dtype=jnp.int32)
    return targets[:, None] == seat_index[None, :]


def join_stack(held_new, held_cached, upper_half, other_new, other_cached):
    held_new = jnp.where(
        upper_half,
        jnp.concatenate([other_new, held_new], axis=0),
        jnp.concatenate([held_new, other_new], axis=0),
    )
    held_cached = jnp.where(
        upper_half,
        jnp.concatenate([other_cached, held_cached], axis=0),
        jnp.concatenate([held_cached, other_cached], axis=0),
    )
    return (held_new, held_cached)


def unstack_columns(held):
    return held.transpose(1, 0, 2).reshape(held.shape[1], held.shape[0] * held.shape[2])


def body(tokens, lengths, hit_pages, new_owner, w_query, w_keyval, w_out, pool_pages):
    rows_dev = tokens.shape[0]
    tp_count = lax.axis_size("tp")
    pool_count = lax.axis_size("pool")
    tp_rank = lax.axis_index("tp")
    group_rows = rows_dev * tp_count
    query_width = w_query.shape[1]
    part_width = w_keyval.shape[1] // 2
    heads_here = query_width // HD
    sharing = tp_count // KVH
    pages_here = pool_pages.shape[0]
    keyval_local = w_keyval.reshape(w_keyval.shape[0] * 2, part_width)
    pages_flat = pool_pages.reshape(pages_here, pool_pages.shape[1] * pool_pages.shape[2])
    tokens_wide = tokens.astype(jnp.float32)
    normed = (
        tokens_wide
        * lax.rsqrt(jnp.mean(tokens_wide * tokens_wide, axis=1, keepdims=True) + EPSILON)
    ).astype(jnp.bfloat16)
    full_query, full_keyval = in_one_piece((w_query, keyval_local), "pool", 0, 1)
    row_piece = lax.all_gather(normed, "tp", axis=0, tiled=True)
    projected = jnp.concatenate(
        [
            jnp.dot(row_piece, full_query, preferred_element_type=jnp.float32),
            jnp.dot(row_piece, full_keyval, preferred_element_type=jnp.float32),
        ],
        axis=1,
    )
    lengths_row = lengths[0]
    ends_at = jnp.cumsum(lengths_row)
    starts_at = ends_at - lengths_row
    token_index = jnp.arange(group_rows, dtype=jnp.int32)
    request_ids = jnp.sum((token_index[:, None] >= ends_at[None, :]).astype(jnp.int32), axis=1)
    chosen = request_ids[:, None] == jnp.arange(REQS, dtype=jnp.int32)[None, :]
    start_of = jnp.sum(jnp.where(chosen, starts_at[None, :], 0), axis=1)
    positions = token_index - start_of + HITS * PAGE
    queries = rotate(
        projected[:, :query_width].reshape(group_rows, heads_here, HD), positions
    ).astype(jnp.bfloat16)
    keyval_part = projected[:, query_width:].astype(jnp.bfloat16)
    page_ids = hit_pages.reshape(-1)
    count_hits = page_ids.shape[0]
    placed_hits = slot_table(page_ids // pages_here, CAPF, pool_count * CAPF)
    wanted = jnp.sum(jnp.where(placed_hits, (page_ids % pages_here)[:, None], 0), axis=0)
    wanted = wanted.reshape(pool_count, CAPF)
    asked = lax.all_to_all(wanted, "pool", split_axis=0, concat_axis=0, tiled=True)
    found = jnp.take(pages_flat, asked.reshape(-1), axis=0)
    found = found.reshape(asked.shape[0], asked.shape[1], pages_flat.shape[1])
    returned = lax.all_to_all(found, "pool", split_axis=0, concat_axis=0, tiled=True)
    returned = returned.reshape(pool_count * CAPF, PAGE * part_width)
    cached_part = jnp.dot(
        placed_hits.astype(jnp.bfloat16), returned, preferred_element_type=jnp.float32
    ).astype(jnp.bfloat16)
    cached_part = cached_part.reshape(count_hits * PAGE, part_width)
    bit_count = sharing.bit_length() - 1
    held_new = keyval_part[None]
    held_cached = cached_part[None]
    for bit_number in range(bit_count):
        other_new, other_cached = partner((held_new, held_cached), "tp", bit_number)
        upper_half = tp_rank // 2**bit_number % 2 == 1
        held_new, held_cached = join_stack(
            held_new, held_cached, upper_half, other_new, other_cached
        )
    new_head = unstack_columns(held_new)
    cached_head = unstack_columns(held_cached)
    new_keys = (
        rotate(new_head[:, :HD].astype(jnp.float32).reshape(group_rows, 1, HD), positions)
        .astype(jnp.bfloat16)
        .reshape(group_rows, HD)
    )
    stored_head = jnp.concatenate([new_keys, new_head[:, HD:]], axis=1)
    own_columns = lax.dynamic_slice_in_dim(
        stored_head, tp_rank % sharing * part_width, part_width, 1
    )
    page_count = group_rows // PAGE
    page_rows = own_columns.reshape(page_count, PAGE * part_width)
    placed_new = slot_table(new_owner[0], CAPN, pool_count * CAPN).astype(jnp.bfloat16)
    outgoing = jnp.dot(placed_new.T, page_rows, preferred_element_type=jnp.float32).astype(
        jnp.bfloat16
    )
    outgoing = outgoing.reshape(pool_count, CAPN, PAGE * part_width)
    new_store = lax.all_to_all(outgoing, "pool", split_axis=0, concat_axis=0, tiled=True).reshape(
        pool_count * CAPN, 1, PAGE * part_width
    )
    keys_all = jnp.concatenate([cached_head[:, :HD], new_keys], axis=0)
    values_all = jnp.concatenate([cached_head[:, HD:], new_head[:, HD:]], axis=0)
    cached_rows = count_hits * PAGE
    key_request = jnp.concatenate(
        [jnp.arange(cached_rows, dtype=jnp.int32) // (HITS * PAGE), request_ids]
    )
    key_order = jnp.concatenate([jnp.full((cached_rows,), -1, jnp.int32), token_index])
    block_rows = min(group_rows, 512)

    def attend(first_row):
        scores = jnp.einsum(
            "bhd,kd->hbk", queries, keys_all, preferred_element_type=jnp.float32
        ) / math.sqrt(HD)
        visible = (request_ids[:, None] == key_request[None, :]) & (
            key_order[None, :] <= token_index[:, None]
        )
        scores = jnp.where(visible[None], scores, -jnp.inf)
        highest = jnp.max(scores, axis=-1, keepdims=True)
        expanded = jnp.exp(scores - highest)
        weights = (expanded / jnp.sum(expanded, axis=-1, keepdims=True)).astype(jnp.bfloat16)
        blended = jnp.einsum(
            "hbk,kd->bhd", weights, values_all, preferred_element_type=jnp.float32
        ).astype(jnp.bfloat16)
        return blended.reshape(block_rows, query_width)

    attended = lax.map(
        attend, jnp.arange(group_rows // block_rows, dtype=jnp.int32) * block_rows
    ).reshape(group_rows, query_width)
    full_out = lax.all_gather(w_out, "pool", axis=1, tiled=True)
    summed = lax.psum_scatter(
        jnp.dot(attended, full_out, preferred_element_type=jnp.float32).astype(jnp.bfloat16),
        "tp",
        scatter_dimension=0,
        tiled=True,
    ).astype(jnp.float32)
    mixed = tokens_wide + summed
    return (mixed, new_store)


def solution(mesh):
    return jax.shard_map(
        body,
        mesh=mesh,
        in_specs=(
            P(("pool", "tp"), None),
            P("pool", None),
            P("pool", None, None),
            P("pool", None),
            P("pool", "tp"),
            P("pool", "tp"),
            P("tp", "pool"),
            P("pool", "tp", None),
        ),
        out_specs=(P(("pool", "tp"), None), P("pool", "tp", None)),
        check_vma=False,
    )
```

profile of v0, /device:TPU:2, one launch (start us, length us, event | category | flops | bytes accessed | tf_op | source)
XLA Modules:
  0.0 323.8 jit_solution(13723968068413563517)
XLA Ops:
  7.3 1.2 reshape.404
  8.4 2.0 pad_maximum_fusion
  10.6 1.1 fusion.18
  11.7 1.8 fusion.19
  13.6 0.7 all-gather.8.cloned.1.call-update
  14.4 0.2 convert_reduce_fusion.2
  14.6 0.7 all_to_all.12
  15.3 8.5 %all-to-all-start = ((s32[8,1,6]{2,1,0:T(1,128)}), s32[8,1,6]{2,1,0:T(1,128)S(1)}, u32[]{:S(2)}, u32[]{:S(2)}) async-start(s32[8,1,6]{2,1,0:T(1,128)} %bitcast), calls=%async_computation | async-start | bytes 8192 | tf_op jit(solution)/shard_map/all_to_all | solution.py:125
  23.8 0.2 reduce-window.4
  24.2 7.4 %all-to-all-done = s32[8,1,6]{2,1,0:T(1,128)S(1)} async-done(((s32[8,1,6]{2,1,0:T(1,128)}), s32[8,1,6]{2,1,0:T(1,128)S(1)}, u32[]{:S(2)}, u32[]{:S(2)}) %all-to-all-start) | async-done | bytes 224 | tf_op jit(solution)/shard_map/all_to_all | solution.py:125
  31.5 0.5 broadcast.349
  32.0 0.7 reduce.3
  32.8 0.7 gather_fusion
  33.6 0.8 broadcast_select_fusion
  34.4 3.4 %all-to-all-start.1 = ((bf16[8,6,2048]{2,1,0:T(8,128)(2,1)}), bf16[8,6,2048]{2,1,0:T(8,128)(2,1)S(1)}, u32[]{:S(2)}, u32[]{:S(2)}) async-start(bf16[8,6,2048]{2,1,0:T(8,128)(2,1)} %broadcast_select_fusion), calls=%async_computation.1 | async-start | bytes 524288 | tf_op jit(solution)/shard_map/all_to_all | solution.py:128
  37.9 1.5 fusion.8
  39.4 13.0 %all-to-all-done.1 = bf16[8,6,2048]{2,1,0:T(8,128)(2,1)S(1)} async-done(((bf16[8,6,2048]{2,1,0:T(8,128)(2,1)}), bf16[8,6,2048]{2,1,0:T(8,128)(2,1)S(1)}, u32[]{:S(2)}, u32[]{:S(2)}) %all-to-all-start.1) | async-done | bytes 196640 | tf_op jit(solution)/shard_map/all_to_all | solution.py:128
  52.5 0.2 convolution_convert_fusion.2
  52.7 0.2 broadcast_in_dim_reshape.3
  53.1 1.2 collective-permute-done
  54.3 1.7 collective-permute-start.1
  56.0 1.8 multiply_cosine_fusion
  57.8 2.2 collective-permute-done.1
  60.0 0.7 maximum_select_fusion
  60.7 33.0 %all-gather.6.cloned.1.call-done = bf16[8192,320]{1,0:T(8,128)(2,1)} async-done(((bf16[1024,320]{1,0:T(8,128)(2,1)}), bf16[8192,320]{1,0:T(8,128)(2,1)}) %all-gather.6.cloned.1.call-update) | async-done | bytes 5242896 | tf_op jit(solution)/shard_map/all_gather | solution.py:27
  93.7 59.0 %all-gather.4.cloned.1.call-done = bf16[512,8192]{1,0:T(8,128)(2,1)} async-done(((bf16[16,8192]{1,0:T(8,128)(2,1)}), bf16[512,8192]{1,0:T(8,128)(2,1)}) %all-gather.4.cloned.1.call-update) | async-done | bytes 8388624 | tf_op jit(solution)/shard_map/all_gather | solution.py:100
  152.7 6.8 %fusion.15 = bf16[1,512,64]{1,2,0:T(8,128)(2,1)S(1)} fusion(bf16[512,8192]{1,0:T(8,128)(2,1)} %all-gather.4.cloned.1.call-done, bf16[8192,320]{1,0:T(8,128)(2,1)} %all-gather.6.cloned.1.call-done), kind=kOutput, calls=%fused_computation.21 | convolution fusion | flops 536903680 | bytes 10551296 | tf_op jit(solution)/shard_map/dot_general | solution.py:104
  159.4 0.3 collective-permute-start.2
  159.8 4.6 %fusion.1 = f32[512,256]{0,1:T(8,128)S(1)} fusion(bf16[512,8192]{1,0:T(8,128)(2,1)S(1)} %copy-done.1, bf16[8192,320]{1,0:T(8,128)(2,1)} %all-gather.6.cloned.1.call-done), kind=kOutput, calls=%fused_computation.3 | convolution fusion | flops 2147483648 | bytes 13107200 | tf_op jit(solution)/shard_map/dot_general | solution.py:103
  164.4 0.2 copy.58
  164.7 0.2 copy.59
  164.9 0.4 collective-permute-start.3
  165.3 1.9 subtract_convert_fusion
  167.2 3.6 %collective-permute-done.3 = bf16[2,512,64]{1,2,0:T(8,128)(2,1)S(1)} collective-permute-done((bf16[2,512,64]{1,2,0:T(8,128)(2,1)S(1)}, bf16[2,512,64]{1,2,0:T(8,128)(2,1)S(1)}, u32[]{:S(2)}, u32[]{:S(2)}) %collective-permute-start.3) | collective-permute-done | bytes 131104 | tf_op jit(solution)/shard_map/ppermute | solution.py:33
  170.9 1.0 fusion.54
  172.1 1.2 fusion.33
  173.4 4.8 %fusion.56 = (f32[2,512]{1,0:T(2,128)S(1)}, f32[2,512,1024]{1,2,0:T(8,128)}) fusion(pred[512,1024]{0,1:T(8,128)(4,1)} %fusion.8, bf16[512,64]{1,0:T(8,128)(2,1)S(1)} %get-tuple-element.25, bf16[512,64]{1,0:T(8,128)(2,1)S(1)} %get-tuple-element.24, bf16[512,128]{1,0:T(8,128)(2,1)S(1)} %copy.56, bf16[512,2,64]{2,0,1:T(8,128)(2,1)} %get-tuple-element.21, ...), kind=kOutput, calls=%fused_computation.109 | convolution fusion | flops 273941504 | bytes 5246976 | tf_op jit(solution)/shard_map/while/body/eval_jaxpr/sub | solution.py:182
  178.2 2.7 fusion.11
  180.8 28.1 %all-gather.8.cloned.1.call-done = bf16[256,8192]{1,0:T(8,128)(2,1)} async-done(((bf16[256,1024]{1,0:T(8,128)(2,1)}), bf16[256,8192]{1,0:T(8,128)(2,1)}) %all-gather.8.cloned.1.call-update) | async-done | bytes 4194320 | tf_op jit(solution)/shard_map/all_gather | solution.py:192
  208.9 7.8 %convolution_convert_fusion = bf16[512,8192]{1,0:T(8,128)(2,1)} fusion(bf16[512,256]{0,1:T(8,128)(2,1)S(1)} %bitcast.70, bf16[256,8192]{1,0:T(8,128)(2,1)} %all-gather.8.cloned.1.call-done), kind=kOutput, calls=%fused_computation.2 | convolution fusion | flops 2151677952 | bytes 12845056 | tf_op jit(solution)/shard_map/dot_general | solution.py:194
  216.7 0.6 copy-done.6
  217.3 0.2 convert_reduce_fusion
  218.0 0.2 reshape.412
  218.2 0.3 convolution_convert_fusion.1
  218.5 12.5 %all_to_all.19 = bf16[8,2,2048]{2,1,0:T(2,128)(2,1)S(1)} all-to-all(bf16[8,2,2048]{2,1,0:T(2,128)(2,1)S(1)} %reshape.413), channel_id=1, replica_groups=mesh['pool'=8,'tp'=32] {'pool'}, dimensions={0} | all-to-all | bytes 131072 | tf_op jit(solution)/shard_map/all_to_all | solution.py:161
  231.0 0.7 reshape.414
  231.7 83.8 %reduce-scatter.2.cloned.1.call-done = bf16[16,8192]{1,0:T(8,128)(2,1)} async-done(((bf16[512,8192]{1,0:T(8,128)(2,1)}), bf16[16,8192]{1,0:T(8,128)(2,1)}) %reduce-scatter.2.cloned.1.call-update) | async-done | bytes 262160 | tf_op jit(solution)/shard_map/reduce_scatter | solution.py:193
  315.5 1.8 convert_add_fusion
  (54 shorter events, 1.9 us)
Async XLA Ops:
  7.2 25.6 %copy-start = (bf16[512,1,2048]{2,0,1:T(8,128)(2,1)S(1)}, bf16[512,1,2048]{2,0,1:T(8,128)(2,1)}, u32[]{:S(2)}) copy-start(bf16[512,1,2048]{2,0,1:T(8,128)(2,1)} %param.15) | copy-start | bytes 6291460
  7.2 30.7 %copy-start.3 = (s32[1024]{0:T(1024)S(1)}, s32[1024]{0:T(1024)}, u32[]{:S(2)}) copy-start(s32[1024]{0:T(1024)} %constant.140.clone.1) | copy-start | bytes 12292
  7.2 7.1 %copy-start.4 = (s32[1,4,4]{2,1,0:T(4,128)S(1)}, s32[1,4,4]{2,1,0:T(4,128)}, u32[]{:S(2)}) copy-start(s32[1,4,4]{2,1,0:T(4,128)} %param.10) | copy-start | bytes 196
  7.2 16.6 %copy-start.5 = (s32[1,4]{1,0:T(1,128)S(1)}, s32[1,4]{1,0:T(1,128)}, u32[]{:S(2)}) copy-start(s32[1,4]{1,0:T(1,128)} %param.9) | copy-start | bytes 52
  7.2 86.5 %all-gather.6.cloned.1.call-start = ((), (), s32[]{:S(2)}) async-start(), calls=%async_computation.5 | async-start | bytes 7077888 | tf_op jit(solution)/shard_map/all_gather | solution.py:27
  10.5 142.2 %all-gather.4.cloned.1.call-start = ((), (), s32[]{:S(2)}) async-start(), calls=%async_computation.4 | async-start | bytes 8650752 | tf_op jit(solution)/shard_map/all_gather | solution.py:100
  13.5 195.4 %all-gather.8.cloned.1.call-start = ((), (), s32[]{:S(2)}) async-start(), calls=%async_computation.6 | async-start | bytes 4718592 | tf_op jit(solution)/shard_map/all_gather | solution.py:192
  15.3 16.2 %all-to-all-start = ((s32[8,1,6]{2,1,0:T(1,128)}), s32[8,1,6]{2,1,0:T(1,128)S(1)}, u32[]{:S(2)}, u32[]{:S(2)}) async-start(s32[8,1,6]{2,1,0:T(1,128)} %bitcast), calls=%async_computation | async-start | bytes 8192 | tf_op jit(solution)/shard_map/all_to_all | solution.py:125
  34.4 18.0 %all-to-all-start.1 = ((bf16[8,6,2048]{2,1,0:T(8,128)(2,1)}), bf16[8,6,2048]{2,1,0:T(8,128)(2,1)S(1)}, u32[]{:S(2)}, u32[]{:S(2)}) async-start(bf16[8,6,2048]{2,1,0:T(8,128)(2,1)} %broadcast_select_fusion), calls=%async_computation.1 | async-start | bytes 524288 | tf_op jit(solution)/shard_map/all_to_all | solution.py:128
  37.8 277.7 %reduce-scatter.2.cloned.1.call-start = ((), (), s32[]{:S(2)}) async-start(), calls=%async_computation.7 | async-start | bytes 8650752 | tf_op jit(solution)/shard_map/reduce_scatter | solution.py:193
  53.0 1.3 collective-permute-start
  54.3 5.6 %collective-permute-start.1 = (bf16[2,512,64]{1,2,0:T(8,128)(2,1)S(1)}, bf16[2,512,64]{1,2,0:T(8,128)(2,1)S(1)}, u32[]{:S(2)}, u32[]{:S(2)}) collective-permute-start(bf16[2,512,64]{1,2,0:T(8,128)(2,1)S(1)} %maximum_select_fusion.2), channel_id=1, source_target_pairs={{0,2},{1,3},{2,0},{3,1},{4,6},{5,7},{6,4},{7,5},{8,10},{9,11},{10,... | collective-permute-start | bytes 393224 | tf_op jit(solution)/shard_map/ppermute | solution.py:33
  152.7 7.1 %copy-start.1 = (bf16[512,8192]{1,0:T(8,128)(2,1)S(1)}, bf16[512,8192]{1,0:T(8,128)(2,1)}, u32[]{:S(2)}) copy-start(bf16[512,8192]{1,0:T(8,128)(2,1)} %all-gather.4.cloned.1.call-done) | copy-start | bytes 25165828
  159.4 5.4 %collective-permute-start.2 = (bf16[1,512,64]{1,2,0:T(8,128)(2,1)S(1)}, bf16[1,512,64]{1,2,0:T(8,128)(2,1)S(1)}, u32[]{:S(2)}, u32[]{:S(2)}) collective-permute-start(bf16[1,512,64]{1,2,0:T(8,128)(2,1)S(1)} %fusion.15), channel_id=1, source_target_pairs={{0,1},{1,0},{2,3},{3,2},{4,5},{5,4},{6,7},{7,6},{8,9},{9,8},{10,11... | collective-permute-start | bytes 196616 | tf_op jit(solution)/shard_map/ppermute | solution.py:33
  164.9 5.9 %collective-permute-start.3 = (bf16[2,512,64]{1,2,0:T(8,128)(2,1)S(1)}, bf16[2,512,64]{1,2,0:T(8,128)(2,1)S(1)}, u32[]{:S(2)}, u32[]{:S(2)}) collective-permute-start(bf16[2,512,64]{1,2,0:T(8,128)(2,1)S(1)} %maximum_select_fusion.3), channel_id=1, source_target_pairs={{0,2},{1,3},{2,0},{3,1},{4,6},{5,7},{6,4},{7,5},{8,10},{9,11},{10,... | collective-permute-start | bytes 393224 | tf_op jit(solution)/shard_map/ppermute | solution.py:33
  216.7 0.7 copy-start.6
  216.7 98.8 %copy-start.2 = (bf16[16,8192]{1,0:T(8,128)(2,1)S(1)}, bf16[16,8192]{1,0:T(8,128)(2,1)}, u32[]{:S(2)}) copy-start(bf16[16,8192]{1,0:T(8,128)(2,1)} %param.8) | copy-start | bytes 786436
Sparse Core Ops, SparseCore 0:
  10.6 83.0 all-gather.5
  96.2 56.3 all-gather.3
  154.5 54.4 all-gather.7
  216.8 98.6 reduce-scatter.1
where the time goes:
time: 324 us
  waiting for transfers between devices  232 us (72%)
  matrix products  27.1 us (8%)
  other arithmetic  16.5 us (5%)
  starting transfers between devices  14.5 us (4%)
  between operations  14.1 us (4%)
  blocking collectives  12.5 us (4%)
  local copies, waits for them, and re-layouts  7.18 us (2%)
    reduce_scatter x1, waiting for transfers between devices, body(): lax.psum_scatter(jnp.dot(attended, full_out, preferred_element_type=jnp.f...  83.8 us
    all_gather x1, waiting for transfers between devices, body(): row_piece = lax.all_gather(normed, 'tp', axis=0, tiled=True)  59 us
    all_gather x1, waiting for transfers between devices, in_one_piece(): lax.all_gather(both, axis, axis=dim, tiled=True)  33 us
    all_gather x1, waiting for transfers between devices, body(): full_out = lax.all_gather(w_out, 'pool', axis=1, tiled=True)  28.1 us
    all_to_all x1, waiting for transfers between devices, body(): lax.all_to_all(found, 'pool', split_axis=0, concat_axis=0, tiled=True)  13 us
    all_to_all x1, blocking collectives, body(): lax.all_to_all(outgoing, 'pool', split_axis=0, concat_axis=0, tiled=True)  12.5 us
    all_to_all x1, starting transfers between devices, body(): lax.all_to_all(wanted, 'pool', split_axis=0, concat_axis=0, tiled=True)  8.47 us
    dot_general x1, matrix products, body(): jnp.dot(attended, full_out, preferred_element_type=jnp.float32)  7.77 us
  transfers between devices with their start and end apart: 10, of which 9 were waited for; matrix products, arithmetic and copies ran while one was open for 11% of the time, Pallas kernels for 0%

commit v1 on v0

v1 whole, which is shorter than its diff:
```python
import math

import jax
import jax.numpy as jnp
from jax import lax
from jax.experimental import pallas as pl
from jax.experimental.pallas import tpu as pltpu
from jax.sharding import PartitionSpec as P


KVH = 8
HD = 128
PAGE = 32
REQS = 4
HITS = 4
CAPF = 6
CAPN = 2

EPSILON = 1e-06
ROPE_BASE = 1000000.0


F32 = jnp.float32
BF16 = jnp.bfloat16


def dot(a, b):
    return jnp.dot(a, b, preferred_element_type=F32)


ALONG_Y = [[(x * 4 + y) * 2 for y in range(4)] for x in range(4)]
ALONG_X = [[(x * 4 + y) * 2 for x in range(4)] for y in range(4)]
I_GROUPS = ALONG_Y + [[d + 1 for d in group] for group in ALONG_X]


def swap_core(value):
    return lax.ppermute(value, "tp", [(s, s ^ 1) for s in range(lax.axis_size("tp"))])


def along_i(value, e):
    pairs = [(s, s ^ (e << 1 if s % 2 == 0 else e << 3)) for s in range(lax.axis_size("tp"))]
    return lax.ppermute(value, "tp", pairs)


def along_j(value, e):
    pairs = [(s, s ^ (e << 3 if s % 2 == 0 else e << 1)) for s in range(lax.axis_size("tp"))]
    return lax.ppermute(value, "tp", pairs)


def exchange(blocks, groups):
    return lax.all_to_all(
        blocks, "tp", split_axis=0, concat_axis=0, axis_index_groups=groups, tiled=True
    )


ANY = pl.BlockSpec(memory_space=pl.ANY)


STEPS = 8
AHEAD = 2


def project(pieces, weights, cosine, sine, place):
    rows, width = pieces[0].shape
    total, wide = rows * len(pieces), weights.shape[1]
    depth, part, tall = width // STEPS, wide // 4, weights.shape[0] // STEPS
    block_rows = total // 32

    def kernel(place_ref, *refs):
        piece_refs, refs = refs[: len(pieces)], refs[len(pieces) :]
        w_ref, cos_ref, sin_ref, query_ref, keyval_ref, packed_ref = refs[:6]
        held, buffer, query_all, keyval_all, sems = refs[6:]

        def copies(step):
            weight_copy = pltpu.make_async_copy(
                w_ref.at[step * tall : (step + 1) * tall], buffer.at[step], sems.at[step, len(pieces)]
            )
            return [weight_copy] + [
                pltpu.make_async_copy(
                    piece.at[:, step * depth : (step + 1) * depth],
                    held.at[step, n * rows : (n + 1) * rows, :],
                    sems.at[step, n],
                )
                for n, piece in enumerate(piece_refs)
            ]

        for step in range(AHEAD):
            for copy in copies(step):
                copy.start()
        for step in range(STEPS):
            for copy in copies(step):
                copy.wait()
            if step + AHEAD < STEPS:
                for copy in copies(step + AHEAD):
                    copy.start()
            packed = buffer[step, depth:, :]
            keyval = jnp.concatenate([packed[:, n * part : (n + 1) * part] for n in range(4)], axis=0)
            term, small = dot(held[step], buffer[step, :depth, :]), dot(held[step], keyval)
            query_all[...] = term if step == 0 else query_all[...] + term
            keyval_all[...] = small if step == 0 else keyval_all[...] + small

        own_core, own_x, own_y = place_ref[0], place_ref[1], place_ref[2]

        def put(b, carry):
            this_core = own_core ^ (b // 16)
            e, j = b // 4 % 4, b % 4
            across = own_x ^ jnp.where(this_core == 0, j, e)
            down = own_y ^ jnp.where(this_core == 0, e, j)
            source = pl.multiple_of(b * block_rows, block_rows)
            target = pl.multiple_of(((across * 4 + down) * 2 + this_core) * block_rows, block_rows)
            cos = cos_ref[pl.ds(target, block_rows), :]
            sin = sin_ref[pl.ds(target, block_rows), :]
            for h in range(wide // HD):
                at = slice(h * HD, (h + 1) * HD)
                v = query_all[pl.ds(source, block_rows), at]
                turned = v * cos + pltpu.roll(v, HD // 2, 1) * sin
                query_ref[pl.ds(target, block_rows), at] = turned.astype(BF16)
            keyval_ref[pl.ds(target, block_rows), :] = keyval_all[pl.ds(source, block_rows), :].astype(
                BF16
            )
            return carry

        lax.fori_loop(0, 32, put, 0)
        packed_ref[...] = jnp.concatenate(
            [keyval_ref[: total // 2, :], keyval_ref[total // 2 :, :]], axis=1
        )

    return pl.pallas_call(
        kernel,
        in_specs=[pl.BlockSpec(memory_space=pltpu.SMEM)]
        + [ANY] * (len(pieces) + 1)
        + [pl.BlockSpec(memory_space=pltpu.VMEM)] * 2,
        out_shape=[
            jax.ShapeDtypeStruct((total, wide), BF16),
            jax.ShapeDtypeStruct((total, part), BF16),
            jax.ShapeDtypeStruct((total // 2, part * 2), BF16),
        ],
        scratch_shapes=[
            pltpu.VMEM((STEPS, total, depth), BF16),
            pltpu.VMEM((STEPS, tall, wide), BF16),
            pltpu.VMEM((total, wide), F32),
            pltpu.VMEM((total, part), F32),
            pltpu.SemaphoreType.DMA((STEPS, len(pieces) + 1)),
        ],
        name="project",
    )(place, *pieces, weights, cosine, sine)


ROW_BLOCK = 128


def attend(queries, cached_parts, new_parts, cosine, sine, token_request, key_request, place):
    rows, wide = queries.shape
    cached = cached_parts[0].shape[0] * 2
    part = HD // 2
    keys = cached + rows

    def kernel(place_ref, query_ref, *refs):
        cached_refs, new_refs, refs = refs[:4], refs[4:8], refs[8:]
        cos_ref, sin_ref, request_ref, key_request_ref, out_ref, new_key_ref, key_all, value_all = refs
        role = place_ref[3]

        def head(part_refs):
            near = [
                jnp.concatenate([ref[:, :part], ref[:, part:]], axis=0) for ref in part_refs
            ]

            def of(k):
                low = jnp.where(role == k, near[0], near[1])
                high = jnp.where(role == (k ^ 2), near[2], near[3])
                return jnp.where(role // 2 == k // 2, low, high)

            return (
                jnp.concatenate([of(0), of(1)], axis=1),
                jnp.concatenate([of(2), of(3)], axis=1),
            )

        key_all[:cached, :], value_all[:cached, :] = head(cached_refs)
        raw, new_values = head(new_refs)
        raw = raw.astype(F32)
        new_keys = (raw * cos_ref[...] + pltpu.roll(raw, HD // 2, 1) * sin_ref[...]).astype(BF16)
        key_all[cached:, :] = new_keys
        new_key_ref[...] = new_keys
        value_all[cached:, :] = new_values
        for first in range(0, rows, ROW_BLOCK):
            many = cached + first + ROW_BLOCK
            at = slice(first, first + ROW_BLOCK)
            token = first + lax.broadcasted_iota(jnp.int32, (ROW_BLOCK, many), 0)
            order = lax.broadcasted_iota(jnp.int32, (ROW_BLOCK, many), 1) - cached
            visible = (request_ref[at, :] == key_request_ref[:, :many]) & (order <= token)
            for h in range(wide // HD):
                columns = slice(h * HD, (h + 1) * HD)
                scores = lax.dot_general(
                    query_ref[at, columns],
                    key_all[:many, :],
                    (((1,), (1,)), ((), ())),
                    preferred_element_type=F32,
                ) * (1.0 / math.sqrt(HD))
                scores = jnp.where(visible, scores, -jnp.inf)
                expanded = jnp.exp(scores - jnp.max(scores, axis=1, keepdims=True))
                weights = expanded * (1.0 / jnp.sum(expanded, axis=1, keepdims=True))
                out_ref[at, columns] = dot(weights.astype(BF16), value_all[:many, :]).astype(BF16)

    vmem = pl.BlockSpec(memory_space=pltpu.VMEM)
    return pl.pallas_call(
        kernel,
        in_specs=[pl.BlockSpec(memory_space=pltpu.SMEM)] + [vmem] * 13,
        out_shape=[
            jax.ShapeDtypeStruct((rows, wide), BF16),
            jax.ShapeDtypeStruct((rows, HD), BF16),
        ],
        scratch_shapes=[pltpu.VMEM((keys, HD), BF16), pltpu.VMEM((keys, HD), BF16)],
        name="attend",
    )(place, queries, *cached_parts, *new_parts, cosine, sine, token_request, key_request)


def slot_table(owners_row, item_index, capacity, seats):
    earlier_same = (owners_row[:, None] == owners_row[None, :]) & (
        item_index[None, :] < item_index[:, None]
    )
    slots = jnp.sum(earlier_same.astype(jnp.int32), axis=1)
    targets = owners_row * capacity + slots
    seat_index = jnp.arange(seats, dtype=jnp.int32)
    return targets[:, None] == seat_index[None, :]


def block(tokens, lengths, hit_pages, new_owner, w_query, w_keyval, w_out, pool_pages):
    rows_dev, width = tokens.shape
    tp_count = lax.axis_size("tp")
    pool_count = lax.axis_size("pool")
    tp_rank = lax.axis_index("tp")
    core = tp_rank % 2
    first_core = core == 0
    place = jnp.stack([core, tp_rank // 8, tp_rank // 2 % 4, tp_rank % (tp_count // KVH)])
    group_rows = rows_dev * tp_count
    chips = tp_count // 2
    query_width = w_query.shape[1]
    part_width = w_keyval.shape[1] // 2
    sharing = tp_count // KVH
    pages_here = pool_pages.shape[0]
    slice_rows = w_query.shape[0]

    keyval_local = w_keyval.reshape(slice_rows, part_width)
    quarter = slice_rows // 4
    keyval_packed = jnp.concatenate(
        [keyval_local[n * quarter : (n + 1) * quarter] for n in range(4)], axis=1
    )
    gathered = lax.all_gather(
        jnp.concatenate([w_query, keyval_packed], axis=0), "pool", axis=0, tiled=True
    )

    tokens_wide = tokens.astype(F32)
    normed = (
        tokens_wide
        * lax.rsqrt(jnp.mean(tokens_wide * tokens_wide, axis=1, keepdims=True) + EPSILON)
    ).astype(BF16)
    line = jnp.concatenate([normed] + [along_j(normed, e) for e in (1, 2, 3)], axis=0)
    own_rows = [line] + [along_i(line, e) for e in (1, 2, 3)]
    other_rows = [swap_core(piece) for piece in own_rows]
    pieces = own_rows + other_rows

    lengths_row = lengths[0]
    ends_at = jnp.cumsum(lengths_row)
    starts_at = ends_at - lengths_row
    token_index = jnp.arange(group_rows, dtype=jnp.int32)
    request_ids = jnp.sum((token_index[:, None] >= ends_at[None, :]).astype(jnp.int32), axis=1)
    chosen = request_ids[:, None] == jnp.arange(REQS, dtype=jnp.int32)[None, :]
    start_of = jnp.sum(jnp.where(chosen, starts_at[None, :], 0), axis=1)
    positions = token_index - start_of + HITS * PAGE

    page_ids = hit_pages.reshape(-1)
    count_hits = page_ids.shape[0]
    hit_index = jnp.arange(count_hits, dtype=jnp.int32)
    placed_hits = slot_table(page_ids // pages_here, hit_index, CAPF, pool_count * CAPF)
    wanted = jnp.sum(jnp.where(placed_hits, (page_ids % pages_here)[:, None], 0), axis=0)
    wanted = wanted.reshape(pool_count, CAPF)
    asked = lax.all_to_all(wanted, "pool", split_axis=0, concat_axis=0, tiled=True)
    pages_flat = pool_pages.reshape(pages_here, pool_pages.shape[1] * pool_pages.shape[2])
    found = jnp.take(pages_flat, asked.reshape(-1), axis=0, mode="clip")
    found = found.reshape(asked.shape[0], asked.shape[1], pages_flat.shape[1])
    returned = lax.all_to_all(found, "pool", split_axis=0, concat_axis=0, tiled=True)
    returned = returned.reshape(pool_count * CAPF, PAGE * part_width)
    cached_part = dot(placed_hits.astype(BF16), returned).astype(BF16)
    cached_part = cached_part.reshape(count_hits * PAGE, part_width)
    cached_part = jnp.concatenate(
        [cached_part[: count_hits * PAGE // 2], cached_part[count_hits * PAGE // 2 :]], axis=1
    )

    role = tp_rank % sharing

    def around(part):
        return [part] + [
            lax.ppermute(part, "tp", [(s, s ^ e) for s in range(tp_count)]) for e in (1, 2, 3)
        ]

    cached_parts = around(cached_part)

    steps_range = jnp.arange(HD // 2, dtype=F32)
    frequency = ROPE_BASE ** (-2.0 * steps_range / HD)
    angles = positions.astype(F32)[:, None] * frequency[None, :]
    cosine, sine = jnp.cos(angles), jnp.sin(angles)
    cosine = jnp.concatenate([cosine, cosine], axis=1)
    sine = jnp.concatenate([-sine, sine], axis=1)
    queries, keyval_part, keyval_packed = project(pieces, gathered, cosine, sine, place)

    new_parts = around(keyval_packed)
    key_request = jnp.concatenate(
        [jnp.arange(count_hits * PAGE, dtype=jnp.int32) // (HITS * PAGE), request_ids]
    )
    attended, new_keys = attend(
        queries,
        cached_parts,
        new_parts,
        cosine,
        sine,
        request_ids[:, None],
        key_request[None, :],
        place,
    )

    own_columns = jnp.where(
        role == 0,
        new_keys[:, :part_width],
        jnp.where(role == 1, new_keys[:, part_width:], keyval_part),
    )
    page_rows = own_columns.reshape(chips, PAGE * part_width)
    page_index = jnp.arange(chips, dtype=jnp.int32)
    placed_new = slot_table(new_owner[0], page_index, CAPN, pool_count * CAPN).astype(BF16)
    outgoing = dot(placed_new.T, page_rows).astype(BF16)
    outgoing = outgoing.reshape(pool_count, CAPN, PAGE * part_width)
    new_store = lax.all_to_all(outgoing, "pool", split_axis=0, concat_axis=0, tiled=True)
    new_store = new_store.reshape(pool_count * CAPN, 1, PAGE * part_width)

    attended = jnp.concatenate([attended, swap_core(attended)], axis=1)
    attended = jnp.concatenate(
        [attended] + [along_i(attended, e) for e in (1, 2, 3)], axis=1
    )
    half_cols = w_out.shape[1] // 2
    quarter_cols = half_cols // 4
    left, right = w_out[:, :half_cols], w_out[:, half_cols:]
    kept = jnp.where(first_core, left, right)
    given = jnp.where(first_core, right, left)
    out_half = jnp.concatenate([kept, swap_core(given)], axis=0)
    quarters = jnp.concatenate(
        [out_half[:, n * quarter_cols : (n + 1) * quarter_cols] for n in range(4)], axis=0
    )
    out_own = exchange(quarters, I_GROUPS)
    own_i = jnp.where(first_core, tp_rank // 2 % 4, tp_rank // 8)
    depth = 2 * query_width
    out_own = jnp.concatenate(
        [lax.dynamic_slice_in_dim(out_own, (own_i ^ e) * depth, depth, 0) for e in range(4)], axis=0
    )
    full_out = lax.all_gather(out_own, "pool", axis=0, tiled=False)
    part = lax.dot_general(
        attended, full_out, (((1,), (1,)), ((), ())), preferred_element_type=F32
    ).astype(BF16)
    parts = lax.all_to_all(part, "tp", split_axis=0, concat_axis=0, tiled=True)
    parts = parts.reshape(4, 4, 2, rows_dev, pool_count, quarter_cols).astype(F32)
    low = jnp.sum(parts[:, :, 0], axis=0)
    high = jnp.sum(parts[:, :, 1], axis=1)
    summed = jnp.stack([low, high]).transpose(2, 3, 0, 1, 4).reshape(rows_dev, width)
    mixed = tokens_wide + summed.astype(F32)
    return (mixed, new_store)


def solution(mesh):
    return jax.shard_map(
        block,
        mesh=mesh,
        in_specs=(
            P(("pool", "tp"), None),
            P("pool", None),
            P("pool", None, None),
            P("pool", None),
            P("pool", "tp"),
            P("pool", "tp"),
            P("tp", "pool"),
            P("pool", "tp", None),
        ),
        out_specs=(P(("pool", "tp"), None), P("pool", "tp", None)),
        check_vma=False,
    )
```

time: 324 us -> 183 us (0.56)
  the two profiles are of different devices: /device:TPU:2 before, /device:TPU:1 now
where the time goes in v1:
time: 183 us; the launch traced here: 182 us
  starting transfers between devices  62.6 us (34%)
  waiting for transfers between devices  41.7 us (23%)
  local copies, waits for them, and re-layouts  22.1 us (12%)
  Pallas kernels  18.3 us (10%)
  other arithmetic  15.4 us (8%)
  between operations  14.5 us (8%)
  matrix products  7.39 us (4%)
    all_to_all x1, waiting for transfers between devices, block(): parts = lax.all_to_all(part, 'tp', split_axis=0, concat_axis=0, tiled=True)  16.2 us
    ppermute x6, starting transfers between devices, swap_core(): lax.ppermute(value, 'tp', [(s, s ^ 1) for s in range(lax.axis_size('tp'))])  14.2 us
    pallas_call x1, Pallas kernels, project(): pl.pallas_call(kernel, in_specs=[pl.BlockSpec(memory_space=pltpu.SMEM)] +...  12.1 us
    ppermute x6, starting transfers between devices, along_i(): return lax.ppermute(value, 'tp', pairs)  7.8 us
    all_to_all x1, starting transfers between devices, block(): parts = lax.all_to_all(part, 'tp', split_axis=0, concat_axis=0, tiled=True)  7.75 us
    all_gather x1, waiting for transfers between devices, block(): full_out = lax.all_gather(out_own, 'pool', axis=0, tiled=False)  7.65 us
    all_to_all x1, starting transfers between devices, block(): lax.all_to_all(wanted, 'pool', split_axis=0, concat_axis=0, tiled=True)  7.05 us
    all_to_all x1, starting transfers between devices, block(): lax.all_to_all(outgoing, 'pool', split_axis=0, concat_axis=0, tiled=True)  6.93 us
  transfers between devices with their start and end apart: 28, of which 9 were waited for; matrix products, arithmetic and copies ran while one was open for 20% of the time, Pallas kernels for 10%

profile of v1, /device:TPU:1, one launch (start us, length us, event | category | flops | bytes accessed | tf_op | source)
XLA Modules:
  0.0 182.0 jit_solution(219667229418649118)
XLA Ops:
  7.2 1.0 fusion.20
  8.6 2.0 %maximum_maximum_fusion = bf16[1280,256]{1,0:T(8,128)(2,1)} fusion(bf16[256,64]{1,0:T(8,128)(2,1)S(1)} %slice.73, bf16[256,64]{1,0:T(8,128)(2,1)S(1)} %slice.71, bf16[256,64]{1,0:T(8,128)(2,1)S(1)} %slice.69, bf16[256,64]{1,0:T(8,128)(2,1)S(1)} %slice.67, bf16[1024,256]{1,0:T(8,128)(2,1)} %param.12), kind=kLoop, calls=%fused_computation.18 | loop fusion | flops 3276800 | bytes 1310720 | tf_op jit(solution)/shard_map/concatenate | solution.py:249
  10.7 3.3 %collective-permute-start.20 = (bf16[256,512]{1,0:T(8,128)(2,1)S(1)}, bf16[256,512]{1,0:T(8,128)(2,1)S(1)}, u32[]{:S(2)}, u32[]{:S(2)}) collective-permute-start(bf16[256,512]{1,0:T(8,128)(2,1)S(1)} %get-tuple-element.22), channel_id=1, source_target_pairs={{0,1},{1,0},{2,3},{3,2},{4,5},{5,4},{6,7},{7,6},{8,9},{9,8},{10,11... | collective-permute-start | bytes 786440 | tf_op jit(solution)/shard_map/ppermute | solution.py:37
  14.0 1.2 collective-permute-done.20
  15.2 0.8 fusion.7
  16.1 3.6 %all-to-all-start.2 = ((bf16[4,512,128]{2,1,0:T(8,128)(2,1)}), bf16[4,512,128]{2,1,0:T(8,128)(2,1)S(1)}, u32[]{:S(2)}, u32[]{:S(2)}) async-start(bf16[4,512,128]{2,1,0:T(8,128)(2,1)} %bitcast.13), calls=%async_computation.2 | async-start | bytes 1048576 | tf_op jit(solution)/shard_map/all_to_all | solution.py:51
  20.0 6.9 %all-to-all-done.2 = bf16[4,512,128]{2,1,0:T(8,128)(2,1)S(1)} async-done(((bf16[4,512,128]{2,1,0:T(8,128)(2,1)}), bf16[4,512,128]{2,1,0:T(8,128)(2,1)S(1)}, u32[]{:S(2)}, u32[]{:S(2)}) %all-to-all-start.2) | async-done | bytes 524320 | tf_op jit(solution)/shard_map/all_to_all | solution.py:51
  28.0 2.8 %collective-permute-start.1 = (bf16[16,8192]{1,0:T(8,128)(2,1)S(1)}, bf16[16,8192]{1,0:T(8,128)(2,1)S(1)}, u32[]{:S(2)}, u32[]{:S(2)}) collective-permute-start(bf16[16,8192]{1,0:T(8,128)(2,1)S(1)} %fusion.6), channel_id=1, source_target_pairs={{0,16},{1,5},{2,18},{3,7},{4,20},{5,1},{6,22},{7,3},{8,24},{9,13},... | collective-permute-start | bytes 786440 | tf_op jit(solution)/shard_map/ppermute | solution.py:47
  30.8 1.1 collective-permute-start.2
  32.9 7.0 %all-to-all-start = ((s32[8,1,6]{2,1,0:T(1,128)}), s32[8,1,6]{2,1,0:T(1,128)S(1)}, u32[]{:S(2)}, u32[]{:S(2)}) async-start(s32[8,1,6]{2,1,0:T(1,128)} %bitcast.9), calls=%async_computation | async-start | bytes 8192 | tf_op jit(solution)/shard_map/all_to_all | solution.py:277
  41.6 1.3 pad_maximum_fusion.refs_0_
  43.3 1.8 collective-permute-start.4
  45.1 1.7 collective-permute-start.5
  48.3 1.4 gather_fusion
  49.6 1.7 reshape.183
  51.3 6.8 %all-to-all-start.1 = ((bf16[8,6,2048]{2,1,0:T(8,128)(2,1)}), bf16[8,6,2048]{2,1,0:T(8,128)(2,1)}, u32[]{:S(2)}, u32[]{:S(2)}) async-start(bf16[8,6,2048]{2,1,0:T(8,128)(2,1)} %reshape.183), calls=%async_computation.1 | async-start | bytes 524288 | tf_op jit(solution)/shard_map/all_to_all | solution.py:281
  58.1 1.9 %fusion.11 = (f32[512,64]{1,0:T(8,128)}, f32[512,64]{1,0:T(8,128)}, f32[512,64]{1,0:T(8,128)}) fusion(f32[64]{0:T(128)S(1)} %multiply_power_fusion, f32[512]{0:T(512)S(1)} %add_convert_fusion), kind=kLoop, calls=%fused_computation.37 | loop fusion | flops 65536 | bytes 395520 | tf_op jit(solution)/shard_map/neg | solution.py:303
  60.0 4.1 %collective-permute-start.6 = (bf16[64,8192]{1,0:T(8,128)(2,1)S(1)}, bf16[64,8192]{1,0:T(8,128)(2,1)}, u32[]{:S(2)}, u32[]{:S(2)}) collective-permute-start(bf16[64,8192]{1,0:T(8,128)(2,1)S(1)} %pad_maximum_fusion.refs_0_), channel_id=1, source_target_pairs={{0,1},{1,0},{2,3},{3,2},{4,5},{5,4},{6,7},{7,6},{8,9},{9,8},{10,11... | collective-permute-start | bytes 3145736 | tf_op jit(solution)/shard_map/ppermute | solution.py:37
  64.2 4.8 %collective-permute-done.4.refs_2_ = bf16[64,8192]{1,0:T(8,128)(2,1)} collective-permute-done((bf16[64,8192]{1,0:T(8,128)(2,1)S(1)}, bf16[64,8192]{1,0:T(8,128)(2,1)}, u32[]{:S(2)}, u32[]{:S(2)}) %collective-permute-start.4) | collective-permute-done | bytes 1048608 | tf_op jit(solution)/shard_map/ppermute | solution.py:42
  68.9 3.6 %collective-permute-start.8 = (bf16[64,8192]{1,0:T(8,128)(2,1)}, bf16[64,8192]{1,0:T(8,128)(2,1)}, u32[]{:S(2)}, u32[]{:S(2)}) collective-permute-start(bf16[64,8192]{1,0:T(8,128)(2,1)} %collective-permute-done.4.refs_2_), channel_id=1, source_target_pairs={{0,1},{1,0},{2,3},{3,2},{4,5},{5,4},{6,7},{7,6},{8,9},{9,8},{10,11... | collective-permute-start | bytes 3145736 | tf_op jit(solution)/shard_map/ppermute | solution.py:37
  72.6 3.1 %collective-permute-start.9 = (bf16[64,8192]{1,0:T(8,128)(2,1)}, bf16[64,8192]{1,0:T(8,128)(2,1)}, u32[]{:S(2)}, u32[]{:S(2)}) collective-permute-start(bf16[64,8192]{1,0:T(8,128)(2,1)} %collective-permute-done.5.refs_3_), channel_id=1, source_target_pairs={{0,1},{1,0},{2,3},{3,2},{4,5},{5,4},{6,7},{7,6},{8,9},{9,8},{10,11... | collective-permute-start | bytes 3145736 | tf_op jit(solution)/shard_map/ppermute | solution.py:37
  75.7 0.8 copy.18.refs_10_
  76.6 2.2 %pad_maximum_fusion.3 = (f32[512,128]{1,0:T(8,128)}, f32[512,128]{1,0:T(8,128)}) fusion(f32[512,64]{1,0:T(8,128)} %get-tuple-element.35, f32[512,64]{1,0:T(8,128)} %get-tuple-element.34, f32[512,64]{1,0:T(8,128)} %get-tuple-element.33), kind=kLoop, calls=%fused_computation.27 | loop fusion | flops 131072 | bytes 917504 | tf_op jit(solution)/shard_map/concatenate | solution.py:302
  78.8 1.7 reshape.184
  80.5 1.1 convolution_convert_fusion.1
  82.5 0.9 pad_maximum_fusion.5.refs_0_
  84.2 2.1 %collective-permute-start.12 = (bf16[256,128]{1,0:T(8,128)(2,1)S(1)}, bf16[256,128]{1,0:T(8,128)(2,1)S(1)}, u32[]{:S(2)}, u32[]{:S(2)}) collective-permute-start(bf16[256,128]{1,0:T(8,128)(2,1)S(1)} %pad_maximum_fusion.5.refs_0_), channel_id=1, source_target_pairs={{0,3},{1,2},{2,1},{3,0},{4,7},{5,6},{6,5},{7,4},{8,11},{9,10},{10,... | collective-permute-start | bytes 196616 | tf_op jit(solution)/shard_map/ppermute | solution.py:293
  86.3 12.1 %project.1 = (bf16[512,256]{1,0:T(8,128)(2,1)}, bf16[512,64]{1,0:T(8,128)(2,1)}, bf16[256,128]{1,0:T(8,128)(2,1)}) custom-call(s32[4]{0:T(128)} %pad_add_fusion.1.place_ref, bf16[64,8192]{1,0:T(8,128)(2,1)} %copy-done.1, bf16[64,8192]{1,0:T(8,128)(2,1)} %collective-permute-done.3.refs_1_, bf16[64,8192]{1,0:T(8,128)(2,1)} %collective-permute-done.4.refs_2_, ...), custom_call_target="tpu_custom_call" | custom-call | tf_op jit(solution)/shard_map/project/pallas_call | solution.py:128
  99.0 1.7 collective-permute-start.15
  101.3 1.0 collective-permute-done.14.refs_6_
  102.3 2.1 %collective-permute-done.15.refs_7_ = bf16[256,128]{1,0:T(8,128)(2,1)S(1)} collective-permute-done((bf16[256,128]{1,0:T(8,128)(2,1)}, bf16[256,128]{1,0:T(8,128)(2,1)S(1)}, u32[]{:S(2)}, u32[]{:S(2)}) %collective-permute-start.15) | collective-permute-done | bytes 65568 | tf_op jit(solution)/shard_map/ppermute | solution.py:293
  105.1 6.2 %attend.1 = (bf16[512,256]{1,0:T(8,128)(2,1)}, bf16[512,128]{1,0:T(8,128)(2,1)}) custom-call(s32[4]{0:T(128)} %pad_add_fusion.1.place_ref, bf16[512,256]{1,0:T(8,128)(2,1)} %get-tuple-element.7.query_ref, bf16[256,128]{1,0:T(8,128)(2,1)} %copy-done.5, bf16[256,128]{1,0:T(8,128)(2,1)} %copy-done.8, bf16[256,128]{1,0:T(8,128)(2,1)} %copy-done.9, ...), custom_call_target="tpu_custom_call" | custom-call | tf_op jit(solution)/shard_map/attend/pallas_call | solution.py:205
  111.5 1.8 %constant_dynamic-update-slice_fusion.1 = (bf16[512,512]{1,0:T(8,128)(2,1)}, bf16[512,2048]{1,0:T(8,128)(2,1)}) fusion(bf16[512,256]{1,0:T(8,128)(2,1)} %get-tuple-element.9), kind=kLoop, calls=%fused_computation.40 | loop fusion | bytes 786432
  113.3 0.9 constant_dynamic-update-slice_fusion
  114.6 3.3 %collective-permute-start.18 = (bf16[512,512]{1,0:T(8,128)(2,1)}, bf16[512,512]{1,0:T(8,128)(2,1)}, u32[]{:S(2)}, u32[]{:S(2)}) collective-permute-start(bf16[512,512]{1,0:T(8,128)(2,1)} %get-tuple-element.23), channel_id=1, source_target_pairs={{0,4},{1,17},{2,6},{3,19},{4,0},{5,21},{6,2},{7,23},{8,12},{9,25},... | collective-permute-start | bytes 1572872 | tf_op jit(solution)/shard_map/ppermute | solution.py:42
  118.0 1.1 select_select_fusion
  119.9 1.1 convolution_convert_fusion
  121.7 6.9 %all-to-all-start.4 = ((bf16[8,2,2048]{2,1,0:T(2,128)(2,1)}), bf16[8,2,2048]{2,1,0:T(2,128)(2,1)S(1)}, u32[]{:S(2)}, u32[]{:S(2)}) async-start(bf16[8,2,2048]{2,1,0:T(2,128)(2,1)} %reshape.187), calls=%async_computation.4 | async-start | bytes 131072 | tf_op jit(solution)/shard_map/all_to_all | solution.py:331
  128.7 0.9 constant_dynamic-update-slice_fusion.4
  129.6 1.1 collective-permute-done.18
  130.7 1.9 %constant_dynamic-update-slice_fusion.3 = bf16[512,2048]{1,0:T(8,128)(2,1)} fusion(bf16[512,2048]{1,0:T(8,128)(2,1)} %constant_dynamic-update-slice_fusion.4, bf16[512,512]{1,0:T(8,128)(2,1)} %collective-permute-done.18), kind=kLoop, calls=%fused_computation.42 | loop fusion | bytes 1048576
  133.3 0.9 constant_dynamic-update-slice_fusion.2
  134.2 7.7 %all-gather.6.cloned.1.call-done = bf16[16384,128]{1,0:T(8,128)(2,1)} async-done(((bf16[2048,128]{1,0:T(8,128)(2,1)}), bf16[16384,128]{1,0:T(8,128)(2,1)}) %all-gather.6.cloned.1.call-update) | async-done | bytes 4194320 | tf_op jit(solution)/shard_map/all_gather | solution.py:353
  141.8 5.1 %fusion.2 = bf16[512,8,128]{2,0,1:T(8,128)(2,1)S(1)} fusion(bf16[8,2048,128]{2,1,0:T(8,128)(2,1)} %bitcast.47, bf16[512,2048]{1,0:T(8,128)(2,1)} %constant_dynamic-update-slice_fusion.2), kind=kOutput, calls=%fused_computation.5 | convolution fusion | flops 2148007936 | bytes 7340032 | tf_op jit(solution)/shard_map/dot_general | solution.py:354
  147.0 1.7 copy.19
  148.6 7.7 %all-to-all-start.3 = ((bf16[512,8,128]{2,1,0:T(8,128)(2,1)}), bf16[512,8,128]{2,1,0:T(8,128)(2,1)S(1)}, u32[]{:S(2)}, u32[]{:S(2)}) async-start(bf16[512,8,128]{2,1,0:T(8,128)(2,1)} %copy.19), calls=%async_computation.3 | async-start | bytes 2097152 | tf_op jit(solution)/shard_map/all_to_all | solution.py:357
  157.1 16.2 %all-to-all-done.3 = bf16[512,8,128]{2,1,0:T(8,128)(2,1)S(1)} async-done(((bf16[512,8,128]{2,1,0:T(8,128)(2,1)}), bf16[512,8,128]{2,1,0:T(8,128)(2,1)S(1)}, u32[]{:S(2)}, u32[]{:S(2)}) %all-to-all-start.3) | async-done | bytes 1048608 | tf_op jit(solution)/shard_map/all_to_all | solution.py:357
  174.3 0.8 convert_add_fusion
  (113 shorter events, 14.4 us)
Async XLA Ops:
  7.2 41.1 %copy-start = (bf16[512,1,2048]{2,0,1:T(8,128)(2,1)S(1)}, bf16[512,1,2048]{2,0,1:T(8,128)(2,1)}, u32[]{:S(2)}) copy-start(bf16[512,1,2048]{2,0,1:T(8,128)(2,1)} %param.15) | copy-start | bytes 6291460
  7.2 3.5 %copy-start.4 = (bf16[256,1024]{1,0:T(8,128)(2,1)S(1)}, bf16[256,1024]{1,0:T(8,128)(2,1)}, u32[]{:S(2)}) copy-start(bf16[256,1024]{1,0:T(8,128)(2,1)} %param.14) | copy-start | bytes 1572868
  7.2 79.1 %all-gather.4.cloned.1.call-start = ((), (), s32[]{:S(2)}) async-start(), calls=%async_computation.5 | async-start | bytes 5898240 | tf_op jit(solution)/shard_map/all_gather | solution.py:248
  10.7 9.2 %copy-start.2 = (bf16[16,8192]{1,0:T(8,128)(2,1)S(1)}, bf16[16,8192]{1,0:T(8,128)(2,1)}, u32[]{:S(2)}) copy-start(bf16[16,8192]{1,0:T(8,128)(2,1)} %param.8) | copy-start | bytes 786436
  10.7 4.5 %collective-permute-start.20 = (bf16[256,512]{1,0:T(8,128)(2,1)S(1)}, bf16[256,512]{1,0:T(8,128)(2,1)S(1)}, u32[]{:S(2)}, u32[]{:S(2)}) collective-permute-start(bf16[256,512]{1,0:T(8,128)(2,1)S(1)} %get-tuple-element.22), channel_id=1, source_target_pairs={{0,1},{1,0},{2,3},{3,2},{4,5},{5,4},{6,7},{7,6},{8,9},{9,8},{10,11... | collective-permute-start | bytes 786440 | tf_op jit(solution)/shard_map/ppermute | solution.py:37
  16.1 15.8 %copy-start.14 = (s32[1,4,4]{2,1,0:T(4,128)S(1)}, s32[1,4,4]{2,1,0:T(4,128)}, u32[]{:S(2)}) copy-start(s32[1,4,4]{2,1,0:T(4,128)} %param.10) | copy-start | bytes 196
  16.1 23.9 %copy-start.15 = (s32[1,4]{1,0:T(1,128)S(1)}, s32[1,4]{1,0:T(1,128)}, u32[]{:S(2)}) copy-start(s32[1,4]{1,0:T(1,128)} %param.9) | copy-start | bytes 52
  16.1 10.8 %all-to-all-start.2 = ((bf16[4,512,128]{2,1,0:T(8,128)(2,1)}), bf16[4,512,128]{2,1,0:T(8,128)(2,1)S(1)}, u32[]{:S(2)}, u32[]{:S(2)}) async-start(bf16[4,512,128]{2,1,0:T(8,128)(2,1)} %bitcast.13), calls=%async_computation.2 | async-start | bytes 1048576 | tf_op jit(solution)/shard_map/all_to_all | solution.py:51
  19.7 122.1 %all-gather.6.cloned.1.call-start = ((), (), s32[]{:S(2)}) async-start(), calls=%async_computation.6 | async-start | bytes 4718592 | tf_op jit(solution)/shard_map/all_gather | solution.py:353
  27.9 12.3 %copy-start.3 = (bf16[16,8192]{1,0:T(8,128)(2,1)}, bf16[16,8192]{1,0:T(8,128)(2,1)S(1)}, u32[]{:S(2)}) copy-start(bf16[16,8192]{1,0:T(8,128)(2,1)S(1)} %fusion.6) | copy-start | bytes 786436
  27.9 12.2 %collective-permute-start = (bf16[16,8192]{1,0:T(8,128)(2,1)S(1)}, bf16[16,8192]{1,0:T(8,128)(2,1)S(1)}, u32[]{:S(2)}, u32[]{:S(2)}) collective-permute-start(bf16[16,8192]{1,0:T(8,128)(2,1)S(1)} %fusion.6), channel_id=1, source_target_pairs={{0,8},{1,3},{2,10},{3,1},{4,12},{5,7},{6,14},{7,5},{8,0},{9,11},{1... | collective-permute-start | bytes 786440 | tf_op jit(solution)/shard_map/ppermute | solution.py:47
  28.0 12.2 %collective-permute-start.1 = (bf16[16,8192]{1,0:T(8,128)(2,1)S(1)}, bf16[16,8192]{1,0:T(8,128)(2,1)S(1)}, u32[]{:S(2)}, u32[]{:S(2)}) collective-permute-start(bf16[16,8192]{1,0:T(8,128)(2,1)S(1)} %fusion.6), channel_id=1, source_target_pairs={{0,16},{1,5},{2,18},{3,7},{4,20},{5,1},{6,22},{7,3},{8,24},{9,13},... | collective-permute-start | bytes 786440 | tf_op jit(solution)/shard_map/ppermute | solution.py:47
  30.8 10.8 %collective-permute-start.2 = (bf16[16,8192]{1,0:T(8,128)(2,1)S(1)}, bf16[16,8192]{1,0:T(8,128)(2,1)}, u32[]{:S(2)}, u32[]{:S(2)}) collective-permute-start(bf16[16,8192]{1,0:T(8,128)(2,1)S(1)} %fusion.6), channel_id=1, source_target_pairs={{0,24},{1,7},{2,26},{3,5},{4,28},{5,3},{6,30},{7,1},{8,16},{9,15},... | collective-permute-start | bytes 786440 | tf_op jit(solution)/shard_map/ppermute | solution.py:47
  32.9 14.0 %all-to-all-start = ((s32[8,1,6]{2,1,0:T(1,128)}), s32[8,1,6]{2,1,0:T(1,128)S(1)}, u32[]{:S(2)}, u32[]{:S(2)}) async-start(s32[8,1,6]{2,1,0:T(1,128)} %bitcast.9), calls=%async_computation | async-start | bytes 8192 | tf_op jit(solution)/shard_map/all_to_all | solution.py:277
  40.2 0.7 copy-start.6
  40.9 0.7 copy-start.7
  42.8 35.9 %copy-start.1 = (bf16[64,8192]{1,0:T(8,128)(2,1)}, bf16[64,8192]{1,0:T(8,128)(2,1)S(1)}, u32[]{:S(2)}) copy-start(bf16[64,8192]{1,0:T(8,128)(2,1)S(1)} %pad_maximum_fusion.refs_0_) | copy-start | bytes 3145732
  42.8 21.2 %collective-permute-start.3 = (bf16[64,8192]{1,0:T(8,128)(2,1)S(1)}, bf16[64,8192]{1,0:T(8,128)(2,1)}, u32[]{:S(2)}, u32[]{:S(2)}) collective-permute-start(bf16[64,8192]{1,0:T(8,128)(2,1)S(1)} %pad_maximum_fusion.refs_0_), channel_id=1, source_target_pairs={{0,2},{1,9},{2,0},{3,11},{4,6},{5,13},{6,4},{7,15},{8,10},{9,1},{1... | collective-permute-start | bytes 3145736 | tf_op jit(solution)/shard_map/ppermute | solution.py:42
  43.3 25.6 %collective-permute-start.4 = (bf16[64,8192]{1,0:T(8,128)(2,1)S(1)}, bf16[64,8192]{1,0:T(8,128)(2,1)}, u32[]{:S(2)}, u32[]{:S(2)}) collective-permute-start(bf16[64,8192]{1,0:T(8,128)(2,1)S(1)} %pad_maximum_fusion.refs_0_), channel_id=1, source_target_pairs={{0,4},{1,17},{2,6},{3,19},{4,0},{5,21},{6,2},{7,23},{8,12},{9,25},... | collective-permute-start | bytes 3145736 | tf_op jit(solution)/shard_map/ppermute | solution.py:42
  45.1 27.5 %collective-permute-start.5 = (bf16[64,8192]{1,0:T(8,128)(2,1)S(1)}, bf16[64,8192]{1,0:T(8,128)(2,1)}, u32[]{:S(2)}, u32[]{:S(2)}) collective-permute-start(bf16[64,8192]{1,0:T(8,128)(2,1)S(1)} %pad_maximum_fusion.refs_0_), channel_id=1, source_target_pairs={{0,6},{1,25},{2,4},{3,27},{4,2},{5,29},{6,0},{7,31},{8,14},{9,17},... | collective-permute-start | bytes 3145736 | tf_op jit(solution)/shard_map/ppermute | solution.py:42
  51.3 27.4 %all-to-all-start.1 = ((bf16[8,6,2048]{2,1,0:T(8,128)(2,1)}), bf16[8,6,2048]{2,1,0:T(8,128)(2,1)}, u32[]{:S(2)}, u32[]{:S(2)}) async-start(bf16[8,6,2048]{2,1,0:T(8,128)(2,1)} %reshape.183), calls=%async_computation.1 | async-start | bytes 524288 | tf_op jit(solution)/shard_map/all_to_all | solution.py:281
  60.0 24.2 %collective-permute-start.6 = (bf16[64,8192]{1,0:T(8,128)(2,1)S(1)}, bf16[64,8192]{1,0:T(8,128)(2,1)}, u32[]{:S(2)}, u32[]{:S(2)}) collective-permute-start(bf16[64,8192]{1,0:T(8,128)(2,1)S(1)} %pad_maximum_fusion.refs_0_), channel_id=1, source_target_pairs={{0,1},{1,0},{2,3},{3,2},{4,5},{5,4},{6,7},{7,6},{8,9},{9,8},{10,11... | collective-permute-start | bytes 3145736 | tf_op jit(solution)/shard_map/ppermute | solution.py:37
  64.1 20.1 %collective-permute-start.7 = (bf16[64,8192]{1,0:T(8,128)(2,1)}, bf16[64,8192]{1,0:T(8,128)(2,1)}, u32[]{:S(2)}, u32[]{:S(2)}) collective-permute-start(bf16[64,8192]{1,0:T(8,128)(2,1)} %collective-permute-done.3.refs_1_), channel_id=1, source_target_pairs={{0,1},{1,0},{2,3},{3,2},{4,5},{5,4},{6,7},{7,6},{8,9},{9,8},{10,11... | collective-permute-start | bytes 3145736 | tf_op jit(solution)/shard_map/ppermute | solution.py:37
  68.9 17.4 %collective-permute-start.8 = (bf16[64,8192]{1,0:T(8,128)(2,1)}, bf16[64,8192]{1,0:T(8,128)(2,1)}, u32[]{:S(2)}, u32[]{:S(2)}) collective-permute-start(bf16[64,8192]{1,0:T(8,128)(2,1)} %collective-permute-done.4.refs_2_), channel_id=1, source_target_pairs={{0,1},{1,0},{2,3},{3,2},{4,5},{5,4},{6,7},{7,6},{8,9},{9,8},{10,11... | collective-permute-start | bytes 3145736 | tf_op jit(solution)/shard_map/ppermute | solution.py:37
  72.6 13.7 %collective-permute-start.9 = (bf16[64,8192]{1,0:T(8,128)(2,1)}, bf16[64,8192]{1,0:T(8,128)(2,1)}, u32[]{:S(2)}, u32[]{:S(2)}) collective-permute-start(bf16[64,8192]{1,0:T(8,128)(2,1)} %collective-permute-done.5.refs_3_), channel_id=1, source_target_pairs={{0,1},{1,0},{2,3},{3,2},{4,5},{5,4},{6,7},{7,6},{8,9},{9,8},{10,11... | collective-permute-start | bytes 3145736 | tf_op jit(solution)/shard_map/ppermute | solution.py:37
  83.4 15.0 %copy-start.5 = (bf16[256,128]{1,0:T(8,128)(2,1)}, bf16[256,128]{1,0:T(8,128)(2,1)S(1)}, u32[]{:S(2)}) copy-start(bf16[256,128]{1,0:T(8,128)(2,1)S(1)} %pad_maximum_fusion.5.refs_0_) | copy-start | bytes 196612
  83.5 15.5 %collective-permute-start.10 = (bf16[256,128]{1,0:T(8,128)(2,1)S(1)}, bf16[256,128]{1,0:T(8,128)(2,1)S(1)}, u32[]{:S(2)}, u32[]{:S(2)}) collective-permute-start(bf16[256,128]{1,0:T(8,128)(2,1)S(1)} %pad_maximum_fusion.5.refs_0_), channel_id=1, source_target_pairs={{0,1},{1,0},{2,3},{3,2},{4,5},{5,4},{6,7},{7,6},{8,9},{9,8},{10,11... | collective-permute-start | bytes 196616 | tf_op jit(solution)/shard_map/ppermute | solution.py:293
  84.2 17.1 %collective-permute-start.11 = (bf16[256,128]{1,0:T(8,128)(2,1)S(1)}, bf16[256,128]{1,0:T(8,128)(2,1)S(1)}, u32[]{:S(2)}, u32[]{:S(2)}) collective-permute-start(bf16[256,128]{1,0:T(8,128)(2,1)S(1)} %pad_maximum_fusion.5.refs_0_), channel_id=1, source_target_pairs={{0,2},{1,3},{2,0},{3,1},{4,6},{5,7},{6,4},{7,5},{8,10},{9,11},{10,... | collective-permute-start | bytes 196616 | tf_op jit(solution)/shard_map/ppermute | solution.py:293
  84.2 17.1 %collective-permute-start.12 = (bf16[256,128]{1,0:T(8,128)(2,1)S(1)}, bf16[256,128]{1,0:T(8,128)(2,1)S(1)}, u32[]{:S(2)}, u32[]{:S(2)}) collective-permute-start(bf16[256,128]{1,0:T(8,128)(2,1)S(1)} %pad_maximum_fusion.5.refs_0_), channel_id=1, source_target_pairs={{0,3},{1,2},{2,1},{3,0},{4,7},{5,6},{6,5},{7,4},{8,11},{9,10},{10,... | collective-permute-start | bytes 196616 | tf_op jit(solution)/shard_map/ppermute | solution.py:293
  86.3 25.0 %copy-start.16 = (s32[1,16]{1,0:T(1,128)S(1)}, s32[1,16]{1,0:T(1,128)}, u32[]{:S(2)}) copy-start(s32[1,16]{1,0:T(1,128)} %param.11) | copy-start | bytes 196
  98.4 2.9 %collective-permute-start.13 = (bf16[256,128]{1,0:T(8,128)(2,1)}, bf16[256,128]{1,0:T(8,128)(2,1)S(1)}, u32[]{:S(2)}, u32[]{:S(2)}) collective-permute-start(bf16[256,128]{1,0:T(8,128)(2,1)} %get-tuple-element.8.refs_4_), channel_id=1, source_target_pairs={{0,1},{1,0},{2,3},{3,2},{4,5},{5,4},{6,7},{7,6},{8,9},{9,8},{10,11... | collective-permute-start | bytes 196616 | tf_op jit(solution)/shard_map/ppermute | solution.py:293
  98.5 3.8 %collective-permute-start.14 = (bf16[256,128]{1,0:T(8,128)(2,1)}, bf16[256,128]{1,0:T(8,128)(2,1)S(1)}, u32[]{:S(2)}, u32[]{:S(2)}) collective-permute-start(bf16[256,128]{1,0:T(8,128)(2,1)} %get-tuple-element.8.refs_4_), channel_id=1, source_target_pairs={{0,2},{1,3},{2,0},{3,1},{4,6},{5,7},{6,4},{7,5},{8,10},{9,11},{10,... | collective-permute-start | bytes 196616 | tf_op jit(solution)/shard_map/ppermute | solution.py:293
  99.0 5.5 %copy-start.8 = (bf16[256,128]{1,0:T(8,128)(2,1)}, bf16[256,128]{1,0:T(8,128)(2,1)S(1)}, u32[]{:S(2)}) copy-start(bf16[256,128]{1,0:T(8,128)(2,1)S(1)} %collective-permute-done.10.refs_1_) | copy-start | bytes 196612
  99.0 5.5 %collective-permute-start.15 = (bf16[256,128]{1,0:T(8,128)(2,1)}, bf16[256,128]{1,0:T(8,128)(2,1)S(1)}, u32[]{:S(2)}, u32[]{:S(2)}) collective-permute-start(bf16[256,128]{1,0:T(8,128)(2,1)} %get-tuple-element.8.refs_4_), channel_id=1, source_target_pairs={{0,3},{1,2},{2,1},{3,0},{4,7},{5,6},{6,5},{7,4},{8,11},{9,10},{10,... | collective-permute-start | bytes 196616 | tf_op jit(solution)/shard_map/ppermute | solution.py:293
  101.3 3.2 %copy-start.9 = (bf16[256,128]{1,0:T(8,128)(2,1)}, bf16[256,128]{1,0:T(8,128)(2,1)S(1)}, u32[]{:S(2)}) copy-start(bf16[256,128]{1,0:T(8,128)(2,1)S(1)} %collective-permute-done.11.refs_2_) | copy-start | bytes 196612
  101.3 3.2 %copy-start.10 = (bf16[256,128]{1,0:T(8,128)(2,1)}, bf16[256,128]{1,0:T(8,128)(2,1)S(1)}, u32[]{:S(2)}) copy-start(bf16[256,128]{1,0:T(8,128)(2,1)S(1)} %collective-permute-done.12.refs_3_) | copy-start | bytes 196612
  101.3 3.2 %copy-start.11 = (bf16[256,128]{1,0:T(8,128)(2,1)}, bf16[256,128]{1,0:T(8,128)(2,1)S(1)}, u32[]{:S(2)}) copy-start(bf16[256,128]{1,0:T(8,128)(2,1)S(1)} %collective-permute-done.13.refs_5_) | copy-start | bytes 196612
  102.3 2.1 %copy-start.12 = (bf16[256,128]{1,0:T(8,128)(2,1)}, bf16[256,128]{1,0:T(8,128)(2,1)S(1)}, u32[]{:S(2)}) copy-start(bf16[256,128]{1,0:T(8,128)(2,1)S(1)} %collective-permute-done.14.refs_6_) | copy-start | bytes 196612
  104.4 0.6 copy-start.13
  111.3 2.0 %collective-permute-start.16 = (bf16[512,256]{1,0:T(8,128)(2,1)}, bf16[512,256]{1,0:T(8,128)(2,1)S(1)}, u32[]{:S(2)}, u32[]{:S(2)}) collective-permute-start(bf16[512,256]{1,0:T(8,128)(2,1)} %get-tuple-element.9), channel_id=1, source_target_pairs={{0,1},{1,0},{2,3},{3,2},{4,5},{5,4},{6,7},{7,6},{8,9},{9,8},{10,11... | collective-permute-start | bytes 786440 | tf_op jit(solution)/shard_map/ppermute | solution.py:37
  114.2 14.5 %collective-permute-start.17 = (bf16[512,512]{1,0:T(8,128)(2,1)}, bf16[512,512]{1,0:T(8,128)(2,1)S(1)}, u32[]{:S(2)}, u32[]{:S(2)}) collective-permute-start(bf16[512,512]{1,0:T(8,128)(2,1)} %get-tuple-element.23), channel_id=1, source_target_pairs={{0,2},{1,9},{2,0},{3,11},{4,6},{5,13},{6,4},{7,15},{8,10},{9,1},{1... | collective-permute-start | bytes 1572872 | tf_op jit(solution)/shard_map/ppermute | solution.py:42
  114.6 16.1 %collective-permute-start.18 = (bf16[512,512]{1,0:T(8,128)(2,1)}, bf16[512,512]{1,0:T(8,128)(2,1)}, u32[]{:S(2)}, u32[]{:S(2)}) collective-permute-start(bf16[512,512]{1,0:T(8,128)(2,1)} %get-tuple-element.23), channel_id=1, source_target_pairs={{0,4},{1,17},{2,6},{3,19},{4,0},{5,21},{6,2},{7,23},{8,12},{9,25},... | collective-permute-start | bytes 1572872 | tf_op jit(solution)/shard_map/ppermute | solution.py:42
  117.8 15.5 %collective-permute-start.19 = (bf16[512,512]{1,0:T(8,128)(2,1)}, bf16[512,512]{1,0:T(8,128)(2,1)S(1)}, u32[]{:S(2)}, u32[]{:S(2)}) collective-permute-start(bf16[512,512]{1,0:T(8,128)(2,1)} %get-tuple-element.23), channel_id=1, source_target_pairs={{0,6},{1,25},{2,4},{3,27},{4,2},{5,29},{6,0},{7,31},{8,14},{9,17},... | collective-permute-start | bytes 1572872 | tf_op jit(solution)/shard_map/ppermute | solution.py:42
  121.7 26.9 %all-to-all-start.4 = ((bf16[8,2,2048]{2,1,0:T(2,128)(2,1)}), bf16[8,2,2048]{2,1,0:T(2,128)(2,1)S(1)}, u32[]{:S(2)}, u32[]{:S(2)}) async-start(bf16[8,2,2048]{2,1,0:T(2,128)(2,1)} %reshape.187), calls=%async_computation.4 | async-start | bytes 131072 | tf_op jit(solution)/shard_map/all_to_all | solution.py:331
  148.6 24.7 %all-to-all-start.3 = ((bf16[512,8,128]{2,1,0:T(8,128)(2,1)}), bf16[512,8,128]{2,1,0:T(8,128)(2,1)S(1)}, u32[]{:S(2)}, u32[]{:S(2)}) async-start(bf16[512,8,128]{2,1,0:T(8,128)(2,1)} %copy.19), calls=%async_computation.3 | async-start | bytes 2097152 | tf_op jit(solution)/shard_map/all_to_all | solution.py:357
Sparse Core Ops, SparseCore 0:
  10.8 73.9 all-gather.3
  87.1 54.6 all-gather.5

commit v2 on v1

--- a/solution.py
+++ b/solution.py
@@ -214,6 +214,28 @@
     )(place, queries, *cached_parts, *new_parts, cosine, sine, token_request, key_request)
 
 
+def output_columns(attended, weights):
+    count, tall, wide = weights.shape
+    rows = attended.shape[0]
+    pair = 2
+
+    def kernel(attended_ref, weights_ref, out_ref):
+        both = jnp.concatenate([weights_ref[m] for m in range(pair)], axis=1)
+        out_ref[...] = dot(attended_ref[...], both).astype(BF16)
+
+    return pl.pallas_call(
+        kernel,
+        grid=(count // pair,),
+        in_specs=[
+            pl.BlockSpec((rows, tall), lambda k: (0, 0)),
+            pl.BlockSpec((pair, tall, wide), lambda k: (k, 0, 0)),
+        ],
+        out_specs=pl.BlockSpec((rows, pair * wide), lambda k: (0, k)),
+        out_shape=jax.ShapeDtypeStruct((rows, count * wide), BF16),
+        name="output_columns",
+    )(attended, weights)
+
+
 def slot_table(owners_row, item_index, capacity, seats):
     earlier_same = (owners_row[:, None] == owners_row[None, :]) & (
         item_index[None, :] < item_index[:, None]
@@ -351,9 +373,7 @@
         [lax.dynamic_slice_in_dim(out_own, (own_i ^ e) * depth, depth, 0) for e in range(4)], axis=0
     )
     full_out = lax.all_gather(out_own, "pool", axis=0, tiled=False)
-    part = lax.dot_general(
-        attended, full_out, (((1,), (1,)), ((), ())), preferred_element_type=F32
-    ).astype(BF16)
+    part = output_columns(attended, full_out)
     parts = lax.all_to_all(part, "tp", split_axis=0, concat_axis=0, tiled=True)
     parts = parts.reshape(4, 4, 2, rows_dev, pool_count, quarter_cols).astype(F32)
     low = jnp.sum(parts[:, :, 0], axis=0)

time: 183 us -> 182 us (level)
  Pallas kernels: 18.3 us -> 24.5 us
  matrix products: 7.39 us -> 2.24 us
    pallas_call x0 -> x1, Pallas kernels: none -> 6.23 us  [output_columns(): pl.pallas_call(kernel, grid=(count // pair,), in_specs=[pl.BlockSpec((row...]
    dot_general x1 -> x0, matrix products: 5.15 us -> none  [block(): lax.dot_general(attended, full_out, (((1,), (1,)), ((), ())), preferred_e...]
    unnamed x39 -> x38, local copies, waits for them, and re-layouts: 6.81 us -> 6.94 us
  transfers between devices with their start and end apart: 28 -> 28, of which waited for: 9 -> 9; matrix products, arithmetic and copies ran while one was open for 20% -> 17% of each run, Pallas kernels for 10% -> 14%
where the time goes in v2:
time: 182 us; the launch traced here: 181 us
  starting transfers between devices  61.6 us (34%)
  waiting for transfers between devices  42.2 us (23%)
  Pallas kernels  24.5 us (13%)
  local copies, waits for them, and re-layouts  20.7 us (11%)
  other arithmetic  15.1 us (8%)
  between operations  14.5 us (8%)
  matrix products  2.24 us (1%)
    all_to_all x1, waiting for transfers between devices, block(): parts = lax.all_to_all(part, 'tp', split_axis=0, concat_axis=0, tiled=True)  16.2 us
    ppermute x6, starting transfers between devices, swap_core(): lax.ppermute(value, 'tp', [(s, s ^ 1) for s in range(lax.axis_size('tp'))])  14.3 us
    pallas_call x1, Pallas kernels, project(): pl.pallas_call(kernel, in_specs=[pl.BlockSpec(memory_space=pltpu.SMEM)] +...  12.1 us
    ppermute x6, starting transfers between devices, along_i(): return lax.ppermute(value, 'tp', pairs)  7.8 us
    all_gather x1, waiting for transfers between devices, block(): full_out = lax.all_gather(out_own, 'pool', axis=0, tiled=False)  7.69 us
    all_to_all x1, starting transfers between devices, block(): parts = lax.all_to_all(part, 'tp', split_axis=0, concat_axis=0, tiled=True)  7.57 us
    all_to_all x1, starting transfers between devices, block(): lax.all_to_all(wanted, 'pool', split_axis=0, concat_axis=0, tiled=True)  7.05 us
    unnamed x38, local copies, waits for them, and re-layouts  6.94 us
  transfers between devices with their start and end apart: 28, of which 9 were waited for; matrix products, arithmetic and copies ran while one was open for 17% of the time, Pallas kernels for 14%

profile of v2, /device:TPU:1, one launch (start us, length us, event | category | flops | bytes accessed | tf_op | source)
XLA Modules:
  0.0 180.9 jit_solution(11536242650198133297)
XLA Ops:
  7.2 1.0 fusion.15
  8.6 2.0 %maximum_maximum_fusion = bf16[1280,256]{1,0:T(8,128)(2,1)} fusion(bf16[256,64]{1,0:T(8,128)(2,1)S(1)} %slice.73, bf16[256,64]{1,0:T(8,128)(2,1)S(1)} %slice.71, bf16[256,64]{1,0:T(8,128)(2,1)S(1)} %slice.69, bf16[256,64]{1,0:T(8,128)(2,1)S(1)} %slice.67, bf16[1024,256]{1,0:T(8,128)(2,1)} %param.12), kind=kLoop, calls=%fused_computation.15 | loop fusion | flops 3276800 | bytes 1310720 | tf_op jit(solution)/shard_map/concatenate | solution.py:271
  10.7 3.3 %collective-permute-start.20 = (bf16[256,512]{1,0:T(8,128)(2,1)S(1)}, bf16[256,512]{1,0:T(8,128)(2,1)S(1)}, u32[]{:S(2)}, u32[]{:S(2)}) collective-permute-start(bf16[256,512]{1,0:T(8,128)(2,1)S(1)} %get-tuple-element.22), channel_id=1, source_target_pairs={{0,1},{1,0},{2,3},{3,2},{4,5},{5,4},{6,7},{7,6},{8,9},{9,8},{10,11... | collective-permute-start | bytes 786440 | tf_op jit(solution)/shard_map/ppermute | solution.py:37
  14.0 1.2 collective-permute-done.20
  16.1 3.6 %all-to-all-start.2 = ((bf16[4,512,128]{2,1,0:T(8,128)(2,1)}), bf16[4,512,128]{2,1,0:T(8,128)(2,1)S(1)}, u32[]{:S(2)}, u32[]{:S(2)}) async-start(bf16[4,512,128]{2,1,0:T(8,128)(2,1)} %bitcast.12), calls=%async_computation.2 | async-start | bytes 1048576 | tf_op jit(solution)/shard_map/all_to_all | solution.py:51
  20.0 6.9 %all-to-all-done.2 = bf16[4,512,128]{2,1,0:T(8,128)(2,1)S(1)} async-done(((bf16[4,512,128]{2,1,0:T(8,128)(2,1)}), bf16[4,512,128]{2,1,0:T(8,128)(2,1)S(1)}, u32[]{:S(2)}, u32[]{:S(2)}) %all-to-all-start.2) | async-done | bytes 524320 | tf_op jit(solution)/shard_map/all_to_all | solution.py:51
  27.9 1.7 collective-permute-start.2
  29.7 1.6 collective-permute-start
  32.3 7.0 %all-to-all-start = ((s32[8,1,6]{2,1,0:T(1,128)}), s32[8,1,6]{2,1,0:T(1,128)S(1)}, u32[]{:S(2)}, u32[]{:S(2)}) async-start(s32[8,1,6]{2,1,0:T(1,128)} %bitcast.9), calls=%async_computation | async-start | bytes 8192 | tf_op jit(solution)/shard_map/all_to_all | solution.py:299
  41.0 1.3 pad_maximum_fusion.refs_0_
  42.8 1.8 collective-permute-start.4
  44.6 1.6 collective-permute-start.5
  47.7 1.4 gather_fusion
  49.1 1.7 reshape.186
  50.8 6.6 %all-to-all-start.1 = ((bf16[8,6,2048]{2,1,0:T(8,128)(2,1)}), bf16[8,6,2048]{2,1,0:T(8,128)(2,1)}, u32[]{:S(2)}, u32[]{:S(2)}) async-start(bf16[8,6,2048]{2,1,0:T(8,128)(2,1)} %reshape.186), calls=%async_computation.1 | async-start | bytes 524288 | tf_op jit(solution)/shard_map/all_to_all | solution.py:303
  57.4 1.9 %fusion.6 = (f32[512,64]{1,0:T(8,128)}, f32[512,64]{1,0:T(8,128)}, f32[512,64]{1,0:T(8,128)}) fusion(f32[64]{0:T(128)S(1)} %multiply_power_fusion, f32[512]{0:T(512)S(1)} %add_convert_fusion), kind=kLoop, calls=%fused_computation.32 | loop fusion | flops 65536 | bytes 395520 | tf_op jit(solution)/shard_map/neg | solution.py:325
  59.3 4.2 %collective-permute-start.6 = (bf16[64,8192]{1,0:T(8,128)(2,1)S(1)}, bf16[64,8192]{1,0:T(8,128)(2,1)}, u32[]{:S(2)}, u32[]{:S(2)}) collective-permute-start(bf16[64,8192]{1,0:T(8,128)(2,1)S(1)} %pad_maximum_fusion.refs_0_), channel_id=1, source_target_pairs={{0,1},{1,0},{2,3},{3,2},{4,5},{5,4},{6,7},{7,6},{8,9},{9,8},{10,11... | collective-permute-start | bytes 3145736 | tf_op jit(solution)/shard_map/ppermute | solution.py:37
  63.6 4.9 %collective-permute-done.4.refs_2_ = bf16[64,8192]{1,0:T(8,128)(2,1)} collective-permute-done((bf16[64,8192]{1,0:T(8,128)(2,1)S(1)}, bf16[64,8192]{1,0:T(8,128)(2,1)}, u32[]{:S(2)}, u32[]{:S(2)}) %collective-permute-start.4) | collective-permute-done | bytes 1048608 | tf_op jit(solution)/shard_map/ppermute | solution.py:42
  68.4 3.6 %collective-permute-start.8 = (bf16[64,8192]{1,0:T(8,128)(2,1)}, bf16[64,8192]{1,0:T(8,128)(2,1)}, u32[]{:S(2)}, u32[]{:S(2)}) collective-permute-start(bf16[64,8192]{1,0:T(8,128)(2,1)} %collective-permute-done.4.refs_2_), channel_id=1, source_target_pairs={{0,1},{1,0},{2,3},{3,2},{4,5},{5,4},{6,7},{7,6},{8,9},{9,8},{10,11... | collective-permute-start | bytes 3145736 | tf_op jit(solution)/shard_map/ppermute | solution.py:37
  72.0 3.1 %collective-permute-start.9 = (bf16[64,8192]{1,0:T(8,128)(2,1)}, bf16[64,8192]{1,0:T(8,128)(2,1)}, u32[]{:S(2)}, u32[]{:S(2)}) collective-permute-start(bf16[64,8192]{1,0:T(8,128)(2,1)} %collective-permute-done.5.refs_3_), channel_id=1, source_target_pairs={{0,1},{1,0},{2,3},{3,2},{4,5},{5,4},{6,7},{7,6},{8,9},{9,8},{10,11... | collective-permute-start | bytes 3145736 | tf_op jit(solution)/shard_map/ppermute | solution.py:37
  75.1 0.9 copy.15.refs_10_
  76.0 2.2 %pad_maximum_fusion.3 = (f32[512,128]{1,0:T(8,128)}, f32[512,128]{1,0:T(8,128)}) fusion(f32[512,64]{1,0:T(8,128)} %get-tuple-element.35, f32[512,64]{1,0:T(8,128)} %get-tuple-element.34, f32[512,64]{1,0:T(8,128)} %get-tuple-element.33), kind=kLoop, calls=%fused_computation.24 | loop fusion | flops 131072 | bytes 917504 | tf_op jit(solution)/shard_map/concatenate | solution.py:324
  78.2 1.7 reshape.187
  79.9 1.1 convolution_convert_fusion.1
  81.9 0.9 pad_maximum_fusion.5.refs_0_
  83.6 2.1 %collective-permute-start.12 = (bf16[256,128]{1,0:T(8,128)(2,1)S(1)}, bf16[256,128]{1,0:T(8,128)(2,1)S(1)}, u32[]{:S(2)}, u32[]{:S(2)}) collective-permute-start(bf16[256,128]{1,0:T(8,128)(2,1)S(1)} %pad_maximum_fusion.5.refs_0_), channel_id=1, source_target_pairs={{0,3},{1,2},{2,1},{3,0},{4,7},{5,6},{6,5},{7,4},{8,11},{9,10},{10,... | collective-permute-start | bytes 196616 | tf_op jit(solution)/shard_map/ppermute | solution.py:315
  85.7 12.1 %project.1 = (bf16[512,256]{1,0:T(8,128)(2,1)}, bf16[512,64]{1,0:T(8,128)(2,1)}, bf16[256,128]{1,0:T(8,128)(2,1)}) custom-call(s32[4]{0:T(128)} %pad_add_fusion.1.place_ref, bf16[64,8192]{1,0:T(8,128)(2,1)} %copy-done.1, bf16[64,8192]{1,0:T(8,128)(2,1)} %collective-permute-done.3.refs_1_, bf16[64,8192]{1,0:T(8,128)(2,1)} %collective-permute-done.4.refs_2_, ...), custom_call_target="tpu_custom_call" | custom-call | tf_op jit(solution)/shard_map/project/pallas_call | solution.py:128
  98.0 1.0 collective-permute-start.14
  99.0 1.1 collective-permute-start.15
  100.7 1.1 collective-permute-done.14.refs_6_
  101.8 2.3 %collective-permute-done.15.refs_7_ = bf16[256,128]{1,0:T(8,128)(2,1)S(1)} collective-permute-done((bf16[256,128]{1,0:T(8,128)(2,1)}, bf16[256,128]{1,0:T(8,128)(2,1)S(1)}, u32[]{:S(2)}, u32[]{:S(2)}) %collective-permute-start.15) | collective-permute-done | bytes 65568 | tf_op jit(solution)/shard_map/ppermute | solution.py:315
  104.7 6.2 %attend.1 = (bf16[512,256]{1,0:T(8,128)(2,1)}, bf16[512,128]{1,0:T(8,128)(2,1)}) custom-call(s32[4]{0:T(128)} %pad_add_fusion.1.place_ref, bf16[512,256]{1,0:T(8,128)(2,1)} %get-tuple-element.7.query_ref, bf16[256,128]{1,0:T(8,128)(2,1)} %copy-done.5, bf16[256,128]{1,0:T(8,128)(2,1)} %copy-done.8, bf16[256,128]{1,0:T(8,128)(2,1)} %copy-done.9, ...), custom_call_target="tpu_custom_call" | custom-call | tf_op jit(solution)/shard_map/attend/pallas_call | solution.py:205
  111.0 1.8 %constant_dynamic-update-slice_fusion.1 = (bf16[512,512]{1,0:T(8,128)(2,1)}, bf16[512,2048]{1,0:T(8,128)(2,1)}) fusion(bf16[512,256]{1,0:T(8,128)(2,1)} %get-tuple-element.9), kind=kLoop, calls=%fused_computation.35 | loop fusion | bytes 786432
  112.9 0.9 constant_dynamic-update-slice_fusion
  113.7 1.2 collective-permute-start.17
  115.0 2.4 %collective-permute-start.18 = (bf16[512,512]{1,0:T(8,128)(2,1)}, bf16[512,512]{1,0:T(8,128)(2,1)}, u32[]{:S(2)}, u32[]{:S(2)}) collective-permute-start(bf16[512,512]{1,0:T(8,128)(2,1)} %get-tuple-element.23), channel_id=1, source_target_pairs={{0,4},{1,17},{2,6},{3,19},{4,0},{5,21},{6,2},{7,23},{8,12},{9,25},... | collective-permute-start | bytes 1572872 | tf_op jit(solution)/shard_map/ppermute | solution.py:42
  117.6 1.1 select_select_fusion
  119.5 1.1 convolution_convert_fusion
  121.3 6.8 %all-to-all-start.4 = ((bf16[8,2,2048]{2,1,0:T(2,128)(2,1)}), bf16[8,2,2048]{2,1,0:T(2,128)(2,1)S(1)}, u32[]{:S(2)}, u32[]{:S(2)}) async-start(bf16[8,2,2048]{2,1,0:T(2,128)(2,1)} %reshape.190), calls=%async_computation.4 | async-start | bytes 131072 | tf_op jit(solution)/shard_map/all_to_all | solution.py:353
  128.1 0.9 constant_dynamic-update-slice_fusion.4
  129.0 1.3 collective-permute-done.18
  130.2 1.9 %constant_dynamic-update-slice_fusion.3 = bf16[512,2048]{1,0:T(8,128)(2,1)} fusion(bf16[512,2048]{1,0:T(8,128)(2,1)} %constant_dynamic-update-slice_fusion.4, bf16[512,512]{1,0:T(8,128)(2,1)} %collective-permute-done.18), kind=kLoop, calls=%fused_computation.37 | loop fusion | bytes 1048576
  132.9 0.9 constant_dynamic-update-slice_fusion.2.attended_ref
  133.8 7.7 %all-gather.6.cloned.1.call-done = bf16[16384,128]{1,0:T(8,128)(2,1)} async-done(((bf16[2048,128]{1,0:T(8,128)(2,1)}), bf16[16384,128]{1,0:T(8,128)(2,1)}) %all-gather.6.cloned.1.call-update) | async-done | bytes 4194320 | tf_op jit(solution)/shard_map/all_gather | solution.py:375
  141.4 6.2 %output_columns.1 = bf16[512,1024]{1,0:T(8,128)(2,1)} custom-call(bf16[512,2048]{1,0:T(8,128)(2,1)} %constant_dynamic-update-slice_fusion.2.attended_ref, bf16[8,2048,128]{2,1,0:T(8,128)(2,1)} %bitcast.35), custom_call_target="tpu_custom_call" | custom-call | tf_op jit(solution)/shard_map/output_columns/pallas_call | solution.py:226
  147.7 7.6 %all-to-all-start.3 = ((bf16[32,16,1024]{2,1,0:T(8,128)(2,1)}), bf16[32,16,1024]{2,1,0:T(8,128)(2,1)S(1)}, u32[]{:S(2)}, u32[]{:S(2)}) async-start(bf16[32,16,1024]{2,1,0:T(8,128)(2,1)} %bitcast.36), calls=%async_computation.3 | async-start | bytes 2097152 | tf_op jit(solution)/shard_map/all_to_all | solution.py:377
  155.9 16.2 %all-to-all-done.3 = bf16[32,16,1024]{2,1,0:T(8,128)(2,1)S(1)} async-done(((bf16[32,16,1024]{2,1,0:T(8,128)(2,1)}), bf16[32,16,1024]{2,1,0:T(8,128)(2,1)S(1)}, u32[]{:S(2)}, u32[]{:S(2)}) %all-to-all-start.3) | async-done | bytes 1048608 | tf_op jit(solution)/shard_map/all_to_all | solution.py:377
  173.2 0.8 convert_add_fusion
  (110 shorter events, 14.5 us)
Async XLA Ops:
  7.2 40.5 %copy-start = (bf16[512,1,2048]{2,0,1:T(8,128)(2,1)S(1)}, bf16[512,1,2048]{2,0,1:T(8,128)(2,1)}, u32[]{:S(2)}) copy-start(bf16[512,1,2048]{2,0,1:T(8,128)(2,1)} %param.15) | copy-start | bytes 6291460
  7.2 3.5 %copy-start.4 = (bf16[256,1024]{1,0:T(8,128)(2,1)S(1)}, bf16[256,1024]{1,0:T(8,128)(2,1)}, u32[]{:S(2)}) copy-start(bf16[256,1024]{1,0:T(8,128)(2,1)} %param.14) | copy-start | bytes 1572868
  7.2 78.5 %all-gather.4.cloned.1.call-start = ((), (), s32[]{:S(2)}) async-start(), calls=%async_computation.5 | async-start | bytes 5898240 | tf_op jit(solution)/shard_map/all_gather | solution.py:270
  10.7 9.2 %copy-start.2 = (bf16[16,8192]{1,0:T(8,128)(2,1)S(1)}, bf16[16,8192]{1,0:T(8,128)(2,1)}, u32[]{:S(2)}) copy-start(bf16[16,8192]{1,0:T(8,128)(2,1)} %param.8) | copy-start | bytes 786436
  10.7 4.5 %collective-permute-start.20 = (bf16[256,512]{1,0:T(8,128)(2,1)S(1)}, bf16[256,512]{1,0:T(8,128)(2,1)S(1)}, u32[]{:S(2)}, u32[]{:S(2)}) collective-permute-start(bf16[256,512]{1,0:T(8,128)(2,1)S(1)} %get-tuple-element.22), channel_id=1, source_target_pairs={{0,1},{1,0},{2,3},{3,2},{4,5},{5,4},{6,7},{7,6},{8,9},{9,8},{10,11... | collective-permute-start | bytes 786440 | tf_op jit(solution)/shard_map/ppermute | solution.py:37
  16.1 15.2 %copy-start.14 = (s32[1,4,4]{2,1,0:T(4,128)S(1)}, s32[1,4,4]{2,1,0:T(4,128)}, u32[]{:S(2)}) copy-start(s32[1,4,4]{2,1,0:T(4,128)} %param.10) | copy-start | bytes 196
  16.1 23.3 %copy-start.15 = (s32[1,4]{1,0:T(1,128)S(1)}, s32[1,4]{1,0:T(1,128)}, u32[]{:S(2)}) copy-start(s32[1,4]{1,0:T(1,128)} %param.9) | copy-start | bytes 52
  16.1 10.8 %all-to-all-start.2 = ((bf16[4,512,128]{2,1,0:T(8,128)(2,1)}), bf16[4,512,128]{2,1,0:T(8,128)(2,1)S(1)}, u32[]{:S(2)}, u32[]{:S(2)}) async-start(bf16[4,512,128]{2,1,0:T(8,128)(2,1)} %bitcast.12), calls=%async_computation.2 | async-start | bytes 1048576 | tf_op jit(solution)/shard_map/all_to_all | solution.py:51
  19.7 121.7 %all-gather.6.cloned.1.call-start = ((), (), s32[]{:S(2)}) async-start(), calls=%async_computation.6 | async-start | bytes 4718592 | tf_op jit(solution)/shard_map/all_gather | solution.py:375
  27.9 11.7 %copy-start.3 = (bf16[16,8192]{1,0:T(8,128)(2,1)}, bf16[16,8192]{1,0:T(8,128)(2,1)S(1)}, u32[]{:S(2)}) copy-start(bf16[16,8192]{1,0:T(8,128)(2,1)S(1)} %fusion.1) | copy-start | bytes 786436
  27.9 11.6 %collective-permute-start.2 = (bf16[16,8192]{1,0:T(8,128)(2,1)S(1)}, bf16[16,8192]{1,0:T(8,128)(2,1)S(1)}, u32[]{:S(2)}, u32[]{:S(2)}) collective-permute-start(bf16[16,8192]{1,0:T(8,128)(2,1)S(1)} %fusion.1), channel_id=1, source_target_pairs={{0,24},{1,7},{2,26},{3,5},{4,28},{5,3},{6,30},{7,1},{8,16},{9,15},... | collective-permute-start | bytes 786440 | tf_op jit(solution)/shard_map/ppermute | solution.py:47
  29.6 10.0 %collective-permute-start.1 = (bf16[16,8192]{1,0:T(8,128)(2,1)S(1)}, bf16[16,8192]{1,0:T(8,128)(2,1)S(1)}, u32[]{:S(2)}, u32[]{:S(2)}) collective-permute-start(bf16[16,8192]{1,0:T(8,128)(2,1)S(1)} %fusion.1), channel_id=1, source_target_pairs={{0,16},{1,5},{2,18},{3,7},{4,20},{5,1},{6,22},{7,3},{8,24},{9,13},... | collective-permute-start | bytes 786440 | tf_op jit(solution)/shard_map/ppermute | solution.py:47
  29.7 11.3 %collective-permute-start = (bf16[16,8192]{1,0:T(8,128)(2,1)S(1)}, bf16[16,8192]{1,0:T(8,128)(2,1)}, u32[]{:S(2)}, u32[]{:S(2)}) collective-permute-start(bf16[16,8192]{1,0:T(8,128)(2,1)S(1)} %fusion.1), channel_id=1, source_target_pairs={{0,8},{1,3},{2,10},{3,1},{4,12},{5,7},{6,14},{7,5},{8,0},{9,11},{1... | collective-permute-start | bytes 786440 | tf_op jit(solution)/shard_map/ppermute | solution.py:47
  32.3 14.1 %all-to-all-start = ((s32[8,1,6]{2,1,0:T(1,128)}), s32[8,1,6]{2,1,0:T(1,128)S(1)}, u32[]{:S(2)}, u32[]{:S(2)}) async-start(s32[8,1,6]{2,1,0:T(1,128)} %bitcast.9), calls=%async_computation | async-start | bytes 8192 | tf_op jit(solution)/shard_map/all_to_all | solution.py:299
  39.6 0.7 copy-start.6
  40.3 0.7 copy-start.7
  42.2 36.0 %copy-start.1 = (bf16[64,8192]{1,0:T(8,128)(2,1)}, bf16[64,8192]{1,0:T(8,128)(2,1)S(1)}, u32[]{:S(2)}) copy-start(bf16[64,8192]{1,0:T(8,128)(2,1)S(1)} %pad_maximum_fusion.refs_0_) | copy-start | bytes 3145732
  42.3 21.2 %collective-permute-start.3 = (bf16[64,8192]{1,0:T(8,128)(2,1)S(1)}, bf16[64,8192]{1,0:T(8,128)(2,1)}, u32[]{:S(2)}, u32[]{:S(2)}) collective-permute-start(bf16[64,8192]{1,0:T(8,128)(2,1)S(1)} %pad_maximum_fusion.refs_0_), channel_id=1, source_target_pairs={{0,2},{1,9},{2,0},{3,11},{4,6},{5,13},{6,4},{7,15},{8,10},{9,1},{1... | collective-permute-start | bytes 3145736 | tf_op jit(solution)/shard_map/ppermute | solution.py:42
  42.8 25.6 %collective-permute-start.4 = (bf16[64,8192]{1,0:T(8,128)(2,1)S(1)}, bf16[64,8192]{1,0:T(8,128)(2,1)}, u32[]{:S(2)}, u32[]{:S(2)}) collective-permute-start(bf16[64,8192]{1,0:T(8,128)(2,1)S(1)} %pad_maximum_fusion.refs_0_), channel_id=1, source_target_pairs={{0,4},{1,17},{2,6},{3,19},{4,0},{5,21},{6,2},{7,23},{8,12},{9,25},... | collective-permute-start | bytes 3145736 | tf_op jit(solution)/shard_map/ppermute | solution.py:42
  44.6 27.4 %collective-permute-start.5 = (bf16[64,8192]{1,0:T(8,128)(2,1)S(1)}, bf16[64,8192]{1,0:T(8,128)(2,1)}, u32[]{:S(2)}, u32[]{:S(2)}) collective-permute-start(bf16[64,8192]{1,0:T(8,128)(2,1)S(1)} %pad_maximum_fusion.refs_0_), channel_id=1, source_target_pairs={{0,6},{1,25},{2,4},{3,27},{4,2},{5,29},{6,0},{7,31},{8,14},{9,17},... | collective-permute-start | bytes 3145736 | tf_op jit(solution)/shard_map/ppermute | solution.py:42
  50.8 27.4 %all-to-all-start.1 = ((bf16[8,6,2048]{2,1,0:T(8,128)(2,1)}), bf16[8,6,2048]{2,1,0:T(8,128)(2,1)}, u32[]{:S(2)}, u32[]{:S(2)}) async-start(bf16[8,6,2048]{2,1,0:T(8,128)(2,1)} %reshape.186), calls=%async_computation.1 | async-start | bytes 524288 | tf_op jit(solution)/shard_map/all_to_all | solution.py:303
  59.3 24.3 %collective-permute-start.6 = (bf16[64,8192]{1,0:T(8,128)(2,1)S(1)}, bf16[64,8192]{1,0:T(8,128)(2,1)}, u32[]{:S(2)}, u32[]{:S(2)}) collective-permute-start(bf16[64,8192]{1,0:T(8,128)(2,1)S(1)} %pad_maximum_fusion.refs_0_), channel_id=1, source_target_pairs={{0,1},{1,0},{2,3},{3,2},{4,5},{5,4},{6,7},{7,6},{8,9},{9,8},{10,11... | collective-permute-start | bytes 3145736 | tf_op jit(solution)/shard_map/ppermute | solution.py:37
  63.5 20.1 %collective-permute-start.7 = (bf16[64,8192]{1,0:T(8,128)(2,1)}, bf16[64,8192]{1,0:T(8,128)(2,1)}, u32[]{:S(2)}, u32[]{:S(2)}) collective-permute-start(bf16[64,8192]{1,0:T(8,128)(2,1)} %collective-permute-done.3.refs_1_), channel_id=1, source_target_pairs={{0,1},{1,0},{2,3},{3,2},{4,5},{5,4},{6,7},{7,6},{8,9},{9,8},{10,11... | collective-permute-start | bytes 3145736 | tf_op jit(solution)/shard_map/ppermute | solution.py:37
  68.4 17.3 %collective-permute-start.8 = (bf16[64,8192]{1,0:T(8,128)(2,1)}, bf16[64,8192]{1,0:T(8,128)(2,1)}, u32[]{:S(2)}, u32[]{:S(2)}) collective-permute-start(bf16[64,8192]{1,0:T(8,128)(2,1)} %collective-permute-done.4.refs_2_), channel_id=1, source_target_pairs={{0,1},{1,0},{2,3},{3,2},{4,5},{5,4},{6,7},{7,6},{8,9},{9,8},{10,11... | collective-permute-start | bytes 3145736 | tf_op jit(solution)/shard_map/ppermute | solution.py:37
  72.0 13.7 %collective-permute-start.9 = (bf16[64,8192]{1,0:T(8,128)(2,1)}, bf16[64,8192]{1,0:T(8,128)(2,1)}, u32[]{:S(2)}, u32[]{:S(2)}) collective-permute-start(bf16[64,8192]{1,0:T(8,128)(2,1)} %collective-permute-done.5.refs_3_), channel_id=1, source_target_pairs={{0,1},{1,0},{2,3},{3,2},{4,5},{5,4},{6,7},{7,6},{8,9},{9,8},{10,11... | collective-permute-start | bytes 3145736 | tf_op jit(solution)/shard_map/ppermute | solution.py:37
  82.9 15.0 %copy-start.5 = (bf16[256,128]{1,0:T(8,128)(2,1)}, bf16[256,128]{1,0:T(8,128)(2,1)S(1)}, u32[]{:S(2)}) copy-start(bf16[256,128]{1,0:T(8,128)(2,1)S(1)} %pad_maximum_fusion.5.refs_0_) | copy-start | bytes 196612
  82.9 16.1 %collective-permute-start.10 = (bf16[256,128]{1,0:T(8,128)(2,1)S(1)}, bf16[256,128]{1,0:T(8,128)(2,1)S(1)}, u32[]{:S(2)}, u32[]{:S(2)}) collective-permute-start(bf16[256,128]{1,0:T(8,128)(2,1)S(1)} %pad_maximum_fusion.5.refs_0_), channel_id=1, source_target_pairs={{0,1},{1,0},{2,3},{3,2},{4,5},{5,4},{6,7},{7,6},{8,9},{9,8},{10,11... | collective-permute-start | bytes 196616 | tf_op jit(solution)/shard_map/ppermute | solution.py:315
  83.6 17.1 %collective-permute-start.11 = (bf16[256,128]{1,0:T(8,128)(2,1)S(1)}, bf16[256,128]{1,0:T(8,128)(2,1)S(1)}, u32[]{:S(2)}, u32[]{:S(2)}) collective-permute-start(bf16[256,128]{1,0:T(8,128)(2,1)S(1)} %pad_maximum_fusion.5.refs_0_), channel_id=1, source_target_pairs={{0,2},{1,3},{2,0},{3,1},{4,6},{5,7},{6,4},{7,5},{8,10},{9,11},{10,... | collective-permute-start | bytes 196616 | tf_op jit(solution)/shard_map/ppermute | solution.py:315
  83.6 17.1 %collective-permute-start.12 = (bf16[256,128]{1,0:T(8,128)(2,1)S(1)}, bf16[256,128]{1,0:T(8,128)(2,1)S(1)}, u32[]{:S(2)}, u32[]{:S(2)}) collective-permute-start(bf16[256,128]{1,0:T(8,128)(2,1)S(1)} %pad_maximum_fusion.5.refs_0_), channel_id=1, source_target_pairs={{0,3},{1,2},{2,1},{3,0},{4,7},{5,6},{6,5},{7,4},{8,11},{9,10},{10,... | collective-permute-start | bytes 196616 | tf_op jit(solution)/shard_map/ppermute | solution.py:315
  85.7 25.1 %copy-start.16 = (s32[1,16]{1,0:T(1,128)S(1)}, s32[1,16]{1,0:T(1,128)}, u32[]{:S(2)}) copy-start(s32[1,16]{1,0:T(1,128)} %param.11) | copy-start | bytes 196
  97.9 2.8 %collective-permute-start.13 = (bf16[256,128]{1,0:T(8,128)(2,1)}, bf16[256,128]{1,0:T(8,128)(2,1)S(1)}, u32[]{:S(2)}, u32[]{:S(2)}) collective-permute-start(bf16[256,128]{1,0:T(8,128)(2,1)} %get-tuple-element.8.refs_4_), channel_id=1, source_target_pairs={{0,1},{1,0},{2,3},{3,2},{4,5},{5,4},{6,7},{7,6},{8,9},{9,8},{10,11... | collective-permute-start | bytes 196616 | tf_op jit(solution)/shard_map/ppermute | solution.py:315
  98.0 3.8 %collective-permute-start.14 = (bf16[256,128]{1,0:T(8,128)(2,1)}, bf16[256,128]{1,0:T(8,128)(2,1)S(1)}, u32[]{:S(2)}, u32[]{:S(2)}) collective-permute-start(bf16[256,128]{1,0:T(8,128)(2,1)} %get-tuple-element.8.refs_4_), channel_id=1, source_target_pairs={{0,2},{1,3},{2,0},{3,1},{4,6},{5,7},{6,4},{7,5},{8,10},{9,11},{10,... | collective-permute-start | bytes 196616 | tf_op jit(solution)/shard_map/ppermute | solution.py:315
  99.0 5.1 %copy-start.8 = (bf16[256,128]{1,0:T(8,128)(2,1)}, bf16[256,128]{1,0:T(8,128)(2,1)S(1)}, u32[]{:S(2)}) copy-start(bf16[256,128]{1,0:T(8,128)(2,1)S(1)} %collective-permute-done.10.refs_1_) | copy-start | bytes 196612
  99.0 5.1 %collective-permute-start.15 = (bf16[256,128]{1,0:T(8,128)(2,1)}, bf16[256,128]{1,0:T(8,128)(2,1)S(1)}, u32[]{:S(2)}, u32[]{:S(2)}) collective-permute-start(bf16[256,128]{1,0:T(8,128)(2,1)} %get-tuple-element.8.refs_4_), channel_id=1, source_target_pairs={{0,3},{1,2},{2,1},{3,0},{4,7},{5,6},{6,5},{7,4},{8,11},{9,10},{10,... | collective-permute-start | bytes 196616 | tf_op jit(solution)/shard_map/ppermute | solution.py:315
  100.7 3.4 %copy-start.9 = (bf16[256,128]{1,0:T(8,128)(2,1)}, bf16[256,128]{1,0:T(8,128)(2,1)S(1)}, u32[]{:S(2)}) copy-start(bf16[256,128]{1,0:T(8,128)(2,1)S(1)} %collective-permute-done.11.refs_2_) | copy-start | bytes 196612
  100.7 3.4 %copy-start.10 = (bf16[256,128]{1,0:T(8,128)(2,1)}, bf16[256,128]{1,0:T(8,128)(2,1)S(1)}, u32[]{:S(2)}) copy-start(bf16[256,128]{1,0:T(8,128)(2,1)S(1)} %collective-permute-done.12.refs_3_) | copy-start | bytes 196612
  100.7 3.4 %copy-start.11 = (bf16[256,128]{1,0:T(8,128)(2,1)}, bf16[256,128]{1,0:T(8,128)(2,1)S(1)}, u32[]{:S(2)}) copy-start(bf16[256,128]{1,0:T(8,128)(2,1)S(1)} %collective-permute-done.13.refs_5_) | copy-start | bytes 196612
  101.8 2.3 %copy-start.12 = (bf16[256,128]{1,0:T(8,128)(2,1)}, bf16[256,128]{1,0:T(8,128)(2,1)S(1)}, u32[]{:S(2)}) copy-start(bf16[256,128]{1,0:T(8,128)(2,1)S(1)} %collective-permute-done.14.refs_6_) | copy-start | bytes 196612
  104.0 0.6 copy-start.13
  110.8 2.0 %collective-permute-start.16 = (bf16[512,256]{1,0:T(8,128)(2,1)}, bf16[512,256]{1,0:T(8,128)(2,1)S(1)}, u32[]{:S(2)}, u32[]{:S(2)}) collective-permute-start(bf16[512,256]{1,0:T(8,128)(2,1)} %get-tuple-element.9), channel_id=1, source_target_pairs={{0,1},{1,0},{2,3},{3,2},{4,5},{5,4},{6,7},{7,6},{8,9},{9,8},{10,11... | collective-permute-start | bytes 786440 | tf_op jit(solution)/shard_map/ppermute | solution.py:37
  113.7 14.3 %collective-permute-start.17 = (bf16[512,512]{1,0:T(8,128)(2,1)}, bf16[512,512]{1,0:T(8,128)(2,1)S(1)}, u32[]{:S(2)}, u32[]{:S(2)}) collective-permute-start(bf16[512,512]{1,0:T(8,128)(2,1)} %get-tuple-element.23), channel_id=1, source_target_pairs={{0,2},{1,9},{2,0},{3,11},{4,6},{5,13},{6,4},{7,15},{8,10},{9,1},{1... | collective-permute-start | bytes 1572872 | tf_op jit(solution)/shard_map/ppermute | solution.py:42
  115.0 15.3 %collective-permute-start.18 = (bf16[512,512]{1,0:T(8,128)(2,1)}, bf16[512,512]{1,0:T(8,128)(2,1)}, u32[]{:S(2)}, u32[]{:S(2)}) collective-permute-start(bf16[512,512]{1,0:T(8,128)(2,1)} %get-tuple-element.23), channel_id=1, source_target_pairs={{0,4},{1,17},{2,6},{3,19},{4,0},{5,21},{6,2},{7,23},{8,12},{9,25},... | collective-permute-start | bytes 1572872 | tf_op jit(solution)/shard_map/ppermute | solution.py:42
  117.4 15.5 %collective-permute-start.19 = (bf16[512,512]{1,0:T(8,128)(2,1)}, bf16[512,512]{1,0:T(8,128)(2,1)S(1)}, u32[]{:S(2)}, u32[]{:S(2)}) collective-permute-start(bf16[512,512]{1,0:T(8,128)(2,1)} %get-tuple-element.23), channel_id=1, source_target_pairs={{0,6},{1,25},{2,4},{3,27},{4,2},{5,29},{6,0},{7,31},{8,14},{9,17},... | collective-permute-start | bytes 1572872 | tf_op jit(solution)/shard_map/ppermute | solution.py:42
  121.3 26.4 %all-to-all-start.4 = ((bf16[8,2,2048]{2,1,0:T(2,128)(2,1)}), bf16[8,2,2048]{2,1,0:T(2,128)(2,1)S(1)}, u32[]{:S(2)}, u32[]{:S(2)}) async-start(bf16[8,2,2048]{2,1,0:T(2,128)(2,1)} %reshape.190), calls=%async_computation.4 | async-start | bytes 131072 | tf_op jit(solution)/shard_map/all_to_all | solution.py:353
  147.7 24.5 %all-to-all-start.3 = ((bf16[32,16,1024]{2,1,0:T(8,128)(2,1)}), bf16[32,16,1024]{2,1,0:T(8,128)(2,1)S(1)}, u32[]{:S(2)}, u32[]{:S(2)}) async-start(bf16[32,16,1024]{2,1,0:T(8,128)(2,1)} %bitcast.36), calls=%async_computation.3 | async-start | bytes 2097152 | tf_op jit(solution)/shard_map/all_to_all | solution.py:377
Sparse Core Ops, SparseCore 0:
  10.8 73.8 all-gather.3
  86.5 54.9 all-gather.5
